TPU v7x, 128 devices: a whole 4x4x4 slice. The times are simulated.
128 devices in a mesh: level: 16 (over y_lo, z, core), member: 8 (over y_hi, x).
Axes of the slice: x: 4, y: 4 (y_hi: 2, y_lo: 2; y = y_hi * 2 + y_lo), z: 4, core: 2. Of those that a mesh axis runs over, the one named last changes fastest.
Arguments:
- model_state: float32 [8, 32, 4, 256, 512], P('member', 'level'), may hold values from -6 to 6
- noise_field: bfloat16 [8, 32, 4, 256, 512], P('member', 'level'), may hold values from -5 to 5
- cotangent: bfloat16 [8, 32, 4, 256, 512], P('member', 'level'), may hold values from -6 to 6
- zonal_shift: float32 [32, 4], P('level'), may hold values from -0.02 to 0.02
- viscosity: float32 [32, 4], P('level'), may hold values from 0.1 to 3
- noise_scale: float32 [32, 4], P('level'), may hold values from 0.2 to 1
- w_in: bfloat16 [128, 384], replicated, may hold values from -0.5 to 0.5
- b_in: float32 [384], replicated, may hold values from -3 to 3
- w_mid: bfloat16 [384, 384], replicated, may hold values from -0.3125 to 0.3125
- b_mid: float32 [384], replicated, may hold values from -3 to 3
- w_out: bfloat16 [384, 128], replicated, may hold values from -0.3125 to 0.3125
Outputs:
- next_state: float32 [8, 32, 4, 256, 512], P('member', 'level')
- state_grad: float32 [8, 32, 4, 256, 512], P('member', 'level')
- grad_w_in: float32 [128, 384], P(None, ('level', 'member'))
- grad_w_mid: float32 [384, 384], P(None, ('level', 'member'))
- grad_w_out: float32 [128, 384], P(None, ('level', 'member'))
- grad_bias: float32 [2, 384], P(None, ('level', 'member'))
All inputs are finite; a program needn't handle non-finite values.
Results may differ from a plain program's by a relative error of at most 0.0085.
Values may be sent and summed in bfloat16 or wider, within the bound.
A program may use at most 128 MiB of HBM per device.

v0:
```python
import math

import jax
import jax.numpy as jnp
from jax import lax
from jax.sharding import PartitionSpec as P

WAVES = 128
MODES = 128


def in_one_piece(arrays, axis, split_dim, concat_dim, along):
    ends, at = ([], 0)
    for a in arrays[:-1]:
        at += a.shape[along]
        ends.append(at)
    both = jnp.concatenate(arrays, axis=along)
    return tuple(
        jnp.split(
            lax.all_to_all(both, axis, split_axis=split_dim, concat_axis=concat_dim, tiled=True),
            ends,
            axis=along,
        )
    )


def cut_along(shard, dim, size):
    before, after = (shard.shape[:dim], shard.shape[dim + 1 :])
    return jnp.moveaxis(shard.reshape(*before, size, -1, *after), dim, 0)


def summed_on_arrival(shard, axis, dim):
    size = lax.axis_size(axis)
    tiles = lax.all_to_all(cut_along(shard, dim, size), axis, 0, 0, tiled=True)
    return jnp.sum(tiles, axis=0)


def side_by_side(arrays, axis, dim, along):
    both = jnp.concatenate(arrays, axis=along)
    whole, at, gathered = (summed_on_arrival(both, axis, dim), 0, [])
    for a in arrays:
        gathered.append(lax.slice_in_dim(whole, at, at + a.shape[along], axis=along))
        at += a.shape[along]
    return tuple(gathered)


def spectral_tables(lat_count, lon_count):
    lon_index = jnp.arange(lon_count, dtype=jnp.float32)
    wave_index = jnp.arange(WAVES, dtype=jnp.float32)
    phases = 2.0 * jnp.pi * lon_index[:, None] * wave_index[None, :] / lon_count
    lon_fwd = jnp.concatenate([jnp.cos(phases), jnp.sin(phases)], axis=1)
    wave_weight = jnp.where(wave_index == 0, 1.0, 2.0) / lon_count
    lon_inv = lon_fwd * jnp.concatenate([wave_weight, wave_weight])[None, :]
    lat_index = jnp.arange(lat_count, dtype=jnp.float32)
    mode_index = jnp.arange(MODES, dtype=jnp.float32)
    lat_fwd = jnp.cos(jnp.pi * (lat_index[:, None] + 0.5) * mode_index[None, :] / lat_count)
    lat_inv = lat_fwd * (jnp.where(mode_index == 0, 1.0, 2.0) / lat_count)[None, :]
    return (lon_fwd, lon_inv, lat_fwd, lat_inv)


def spectral_step(fields, zonal_shift, viscosity):
    lon_fwd, lon_inv, lat_fwd, lat_inv = spectral_tables(fields.shape[3], fields.shape[4])
    highest = lax.Precision.HIGHEST
    partial_lon = jnp.einsum("mlfij,jk->mlfik", fields, lon_fwd, precision=highest)
    spectrum = jnp.einsum("mlfik,ip->mlfpk", partial_lon, lat_fwd, precision=highest)
    wave_index = jnp.arange(WAVES, dtype=jnp.float32)
    mode_index = jnp.arange(MODES, dtype=jnp.float32)
    radial = (wave_index / WAVES)[None, :] ** 2 + (mode_index / MODES)[:, None] ** 2
    damping = jnp.exp(-viscosity[:, :, None, None] * radial[None, None])
    phases = zonal_shift[:, :, None, None] * wave_index[None, None, None, :]
    cosine = jnp.cos(phases) * damping
    sine = jnp.sin(phases) * damping
    cos_part = spectrum[..., :WAVES]
    sin_part = spectrum[..., WAVES:]
    rotated = jnp.concatenate(
        [cos_part * cosine - sin_part * sine, cos_part * sine + sin_part * cosine], axis=-1
    )
    halfway = jnp.einsum("mlfpk,ip->mlfik", rotated, lat_inv, precision=highest)
    return jnp.einsum("mlfik,jk->mlfij", halfway, lon_inv, precision=highest)


def silu_slope(values):
    sigmoid = jax.nn.sigmoid(values)
    return sigmoid * (1.0 + values * (1.0 - sigmoid))


def columns_forward(cols_in, w_in, b_in, w_mid, b_mid, w_out):
    col_shape = cols_in.shape
    flat_in = cols_in.reshape(
        col_shape[0], col_shape[1] * col_shape[2], col_shape[3] * col_shape[4]
    )
    pre_one = (
        jnp.einsum("ih,mic->mhc", w_in, flat_in, preferred_element_type=jnp.float32)
        + b_in[None, :, None]
    )
    act_one = jax.nn.silu(pre_one).astype(jnp.bfloat16)
    pre_two = (
        jnp.einsum("ih,mic->mhc", w_mid, act_one, preferred_element_type=jnp.float32)
        + b_mid[None, :, None]
    )
    act_two = jax.nn.silu(pre_two).astype(jnp.bfloat16)
    tendency = jnp.einsum("ho,mhc->moc", w_out, act_two, preferred_element_type=jnp.float32).astype(
        jnp.bfloat16
    )
    return (tendency.reshape(col_shape), (flat_in, pre_one, act_one, pre_two, act_two))


def columns_backward(grad_cols, stored, w_in, w_mid, w_out):
    flat_in, pre_one, act_one, pre_two, act_two = stored
    col_shape = grad_cols.shape
    grad_tend = grad_cols.reshape(flat_in.shape)
    gw_out = jnp.einsum("moc,mhc->oh", grad_tend, act_two, preferred_element_type=jnp.float32)
    slope_two = (
        jnp.einsum("ho,moc->mhc", w_out, grad_tend, preferred_element_type=jnp.float32)
        * silu_slope(pre_two)
    ).astype(jnp.bfloat16)
    gw_mid = jnp.einsum("mic,mhc->ih", act_one, slope_two, preferred_element_type=jnp.float32)
    slope_one = (
        jnp.einsum("ih,mhc->mic", w_mid, slope_two, preferred_element_type=jnp.float32)
        * silu_slope(pre_one)
    ).astype(jnp.bfloat16)
    gw_in = jnp.einsum("mic,mhc->ih", flat_in, slope_one, preferred_element_type=jnp.float32)
    gbias = jnp.stack(
        [
            jnp.sum(slope_one, axis=(0, 2), dtype=jnp.float32),
            jnp.sum(slope_two, axis=(0, 2), dtype=jnp.float32),
        ]
    )
    back_cols = jnp.einsum(
        "ih,mhc->mic", w_in, slope_one, preferred_element_type=jnp.float32
    ).astype(jnp.bfloat16)
    return (back_cols.reshape(col_shape), (gw_in, gw_mid, gw_out, gbias))


def per_device(
    model_state,
    noise_field,
    cotangent,
    zonal_shift,
    viscosity,
    noise_scale,
    w_in,
    b_in,
    w_mid,
    b_mid,
    w_out,
):
    members_here = model_state.shape[0]
    lat_count = model_state.shape[3]
    lon_count = model_state.shape[4]
    dynamics = spectral_step(model_state, zonal_shift, viscosity)
    factor = 1.0 + noise_scale[None, :, :, None, None] * noise_field.astype(jnp.float32)
    inputs_lev = dynamics.astype(jnp.bfloat16)
    grad_lev = (cotangent.astype(jnp.float32) * factor).astype(jnp.bfloat16)
    cols_in, grad_cols = in_one_piece((inputs_lev, grad_lev), "level", 3, 1, 0)
    tend_cols, stored = columns_forward(cols_in, w_in, b_in, w_mid, b_mid, w_out)
    back_cols, weight_grads = columns_backward(grad_cols, stored, w_in, w_mid, w_out)
    tend_lev, back_lev = (
        lax.all_to_all(tend_cols, "level", split_axis=1, concat_axis=3, tiled=True),
        lax.all_to_all(back_cols, "level", split_axis=1, concat_axis=3, tiled=True),
    )
    next_state = dynamics + tend_lev.astype(jnp.float32) * factor
    grad_levels = cotangent.astype(jnp.float32) + back_lev.astype(jnp.float32)
    unused, pullback = jax.vjp(
        lambda fields: spectral_step(fields, zonal_shift, viscosity), model_state
    )
    state_grad = pullback(grad_levels)[0]
    level_sums = side_by_side(
        (weight_grads[0], weight_grads[1], weight_grads[2], weight_grads[3]), "level", 1, 0
    )
    summed = side_by_side(
        (level_sums[0], level_sums[1], level_sums[2], level_sums[3]), "member", 1, 0
    )
    norm_scale = 1.0 / math.sqrt(members_here * lax.axis_size("member") * lat_count * lon_count)
    return (
        next_state,
        state_grad,
        summed[0] * norm_scale,
        summed[1] * norm_scale,
        summed[2] * norm_scale,
        summed[3] * norm_scale,
    )


def solution(mesh):
    return jax.shard_map(
        per_device,
        mesh=mesh,
        in_specs=(
            P("member", "level", None, None, None),
            P("member", "level", None, None, None),
            P("member", "level", None, None, None),
            P("level", None),
            P("level", None),
            P("level", None),
            P(),
            P(),
            P(),
            P(),
            P(),
        ),
        out_specs=(
            P("member", "level", None, None, None),
            P("member", "level", None, None, None),
            P(None, ("level", "member")),
            P(None, ("level", "member")),
            P(None, ("level", "member")),
            P(None, ("level", "member")),
        ),
        check_vma=False,
    )
```

profile of v0, /device:TPU:1, one launch (start us, length us, event | category | flops | bytes accessed | tf_op | source)
XLA Modules:
  0.0 261.1 jit_solution(4293808738096719609)
XLA Ops:
  0.8 0.7 neg.17
  1.4 0.8 fusion.80
  2.4 0.9 fusion.61
  3.3 5.9 %fusion.27 = f32[256,2,4,256]{3,0,2,1:T(8,128)S(1)} fusion(f32[1,2,4,256,512]{4,3,2,1,0:T(8,128)} %param.11, f32[512,128]{0,1:T(8,128)S(1)} %get-tuple-element.33, f32[512,128]{0,1:T(8,128)S(1)} %get-tuple-element.32), kind=kOutput, calls=%fused_computation.46 | convolution fusion | flops 3221356544 | bytes 6815744 | tf_op jit(solution)/shard_map/mlfij,jk->mlfik/dot_general | solution.py:64
  9.2 2.8 %fusion.36 = f32[1,2,4,128,256]{4,3,2,1,0:T(8,128)S(1)} fusion(f32[256,2,4,256]{3,0,2,1:T(8,128)S(1)} %fusion.27, f32[256]{0:T(256)S(1)} %add_multiply_fusion), kind=kOutput, calls=%fused_computation.59 | convolution fusion | flops 805371904 | bytes 3146752 | tf_op jit(solution)/shard_map/mlfik,ip->mlfpk/dot_general | solution.py:65
  12.4 2.3 fusion.42
  14.7 3.6 %fusion.32 = f32[2,4,256,512]{3,2,1,0:T(8,128)S(1)} fusion(f32[256,2,4,256]{3,0,2,1:T(8,128)S(1)} %fusion.42, f32[256]{0:T(256)S(1)} %pad_maximum_fusion.6, f32[512,128]{0,1:T(8,128)S(1)} %get-tuple-element.33, f32[512,128]{0,1:T(8,128)S(1)} %get-tuple-element.32), kind=kOutput, calls=%fused_computation.54 | convolution fusion | flops 3221487616 | bytes 6816768 | tf_op jit(solution)/shard_map/mlfik,jk->mlfij/dot_general | solution.py:79
  18.3 2.0 copy-done.2
  20.6 1.3 copy-done.4
  22.6 0.9 fusion.22
  23.9 3.7 %copy.46 = bf16[2,2,4,256,512]{4,2,1,0,3:T(4,128)(2,1)S(1)} copy(bf16[2,2,4,256,512]{4,3,2,1,0:T(8,128)(2,1)S(1)} %pad_maximum_fusion) | data formatting | bytes 8388608 | tf_op jit(solution)/shard_map/concatenate | solution.py:17
  27.6 56.8 %all_to_all.43 = bf16[2,2,4,256,512]{4,2,1,0,3:T(4,128)(2,1)S(1)} all-to-all(bf16[2,2,4,256,512]{4,2,1,0,3:T(4,128)(2,1)S(1)} %copy.46), channel_id=1, replica_groups=mesh['level'=16,'member'=8] {'level'}, dimensions={3} | all-to-all | bytes 8388608 | tf_op jit(solution)/shard_map/all_to_all | solution.py:20
  84.4 4.5 %copy.86 = bf16[2,2,4,16,16,512]{5,4,2,1,3,0:T(8,128)(2,1)S(1)} copy(bf16[2,2,4,16,16,512]{5,2,1,0,4,3:T(4,128)(2,1)S(1)} %bitcast.239) | data formatting | bytes 8388608 | tf_op jit(solution)/shard_map/all_to_all | solution.py:20
  88.9 1.8 fusion.93
  90.7 4.2 %reshape.262 = bf16[128,8192,1]{1,0,2:T(8,128)(2,1)} reshape(bf16[1,16,2,4,16,512]{5,4,3,2,1,0:T(8,128)(2,1)} %get-tuple-element.25) | data formatting | bytes 4194304 | tf_op jit(solution)/shard_map/reshape.25
  94.9 4.3 %copy.81 = bf16[16,8,16,512]{3,1,2,0:T(8,128)(2,1)} copy(bf16[16,8,16,512]{3,2,1,0:T(8,128)(2,1)} %bitcast.236) | data formatting | bytes 4194304
  99.2 2.3 reshape.264
  101.6 1.4 copy.83
  103.2 6.7 %fusion.11 = (bf16[1,384,8192]{2,1,0:T(8,128)(2,1)S(1)}, f32[1,8192,384]{1,2,0:T(8,128)}) fusion(f32[384]{0:T(512)S(1)} %copy-done.36, bf16[128,8192]{1,0:T(8,128)(2,1)S(1)} %bitcast.250, bf16[128,384]{1,0:T(8,128)(2,1)S(1)} %copy-done.19), kind=kOutput, calls=%fused_computation.20 | convolution fusion | flops 824180736 | bytes 21071360 | tf_op jit(solution)/shard_map/ih,mic->mhc/dot_general | solution.py:93
  109.9 8.1 %fusion.5 = (bf16[1,384,8192]{2,1,0:T(8,128)(2,1)}, f32[1,8192,384]{1,2,0:T(8,128)S(1)}) fusion(f32[384]{0:T(512)S(1)} %copy-done.37, bf16[384,384]{1,0:T(8,128)(2,1)S(1)} %copy-done, bf16[1,384,8192]{2,1,0:T(8,128)(2,1)S(1)} %get-tuple-element.36), kind=kOutput, calls=%fused_computation.10 | convolution fusion | flops 2434793472 | bytes 25462272 | tf_op jit(solution)/shard_map/ih,mic->mhc/dot_general | solution.py:98
  118.0 6.5 %convert_reduce_fusion = (f32[384]{0:T(512)S(1)}, bf16[1,384,8192]{2,1,0:T(8,128)(2,1)S(1)}) fusion(f32[1,8192,384]{1,2,0:T(8,128)S(1)} %get-tuple-element.39, bf16[384,128]{1,0:T(8,128)(2,1)S(1)} %copy-done.20, bf16[128,8192]{1,0:T(8,128)(2,1)S(1)} %bitcast.249), kind=kOutput, calls=%fused_computation.24 | convolution fusion | flops 839908992 | bytes 21071360 | tf_op jit(solution)/shard_map/ho,moc->mhc/dot_general | solution.py:114
  124.5 10.7 %convert_reduce_fusion.1 = (f32[384]{0:T(512)S(1)}, bf16[1,384,8192]{2,1,0:T(8,128)(2,1)}) fusion(f32[1,8192,384]{1,2,0:T(8,128)} %get-tuple-element.37, bf16[384,384]{1,0:T(8,128)(2,1)S(1)} %copy-done, bf16[1,384,8192]{2,1,0:T(8,128)(2,1)S(1)} %get-tuple-element.43), kind=kOutput, calls=%fused_computation.25 | convolution fusion | flops 2450521600 | bytes 25462272 | tf_op jit(solution)/shard_map/ih,mhc->mic/dot_general | solution.py:119
  135.2 3.5 %fusion.16 = f32[384,16,24]{0,2,1:T(8,128)S(1)} fusion(bf16[16,24,8192]{2,1,0:T(8,128)(2,1)S(1)} %bitcast.251, bf16[1,384,8192]{2,1,0:T(8,128)(2,1)S(1)} %copy-done.39), kind=kOutput, calls=%fused_computation.30 | convolution fusion | flops 2415919104 | bytes 13172736 | tf_op jit(solution)/shard_map/mic,mhc->ih/dot_general | solution.py:117
  139.2 4.7 %fusion.94 = f32[128,16,24]{0,2,1:T(8,128)S(1)} fusion(bf16[128,8192,1]{1,0,2:T(8,128)(2,1)S(1)} %copy-done.14, bf16[16,24,8192]{2,1,0:T(8,128)(2,1)} %bitcast.246), kind=kOutput, calls=%fused_computation.131 | convolution fusion | flops 805306368 | bytes 8585216 | tf_op jit(solution)/shard_map/mic,mhc->ih/dot_general | solution.py:122
  144.4 2.0 fusion.95
  146.7 21.0 %all_to_all.44 = f32[16,642,24]{1,2,0:T(8,128)S(1)} all-to-all(f32[16,642,24]{1,2,0:T(8,128)S(1)} %bitcast.248), channel_id=1, replica_groups=mesh['level'=16,'member'=8] {'level'}, dimensions={0} | all-to-all | bytes 1972224 | tf_op jit(solution)/shard_map/all_to_all | solution.py:34
  168.5 6.4 %all-to-all-start.4 = ((f32[8,642,3]{1,2,0:T(4,128)}), f32[8,642,3]{1,2,0:T(4,128)S(1)}, u32[]{:S(2)}, u32[]{:S(2)}) async-start(f32[8,642,3]{1,2,0:T(4,128)} %bitcast.68), calls=%async_computation.4 | async-start | bytes 196608 | tf_op jit(solution)/shard_map/all_to_all | solution.py:34
  174.9 5.9 %fusion.15 = bf16[1,128,8192]{1,2,0:T(8,128)(2,1)} fusion(bf16[128,384]{1,0:T(8,128)(2,1)S(1)} %copy-done.19, bf16[1,384,8192]{2,1,0:T(8,128)(2,1)} %get-tuple-element.41), kind=kOutput, calls=%fused_computation.29 | convolution fusion | flops 806354944 | bytes 8486912 | tf_op jit(solution)/shard_map/ih,mhc->mic/dot_general | solution.py:129
  180.8 2.9 %copy.52 = bf16[1,128,8192]{2,1,0:T(8,128)(2,1)S(1)} copy(bf16[1,128,8192]{1,2,0:T(8,128)(2,1)} %fusion.15) | data formatting | bytes 4194304 | tf_op jit(solution)/shard_map/convert_element_type | solution.py:131
  183.7 2.1 copy.84
  185.9 4.5 %all-to-all-start.2 = ((bf16[1,32,4,16,512]{4,3,2,0,1:T(8,128)(2,1)}), bf16[1,32,4,16,512]{4,3,2,0,1:T(8,128)(2,1)S(1)}, u32[]{:S(2)}, u32[]{:S(2)}) async-start(bf16[1,32,4,16,512]{4,3,2,0,1:T(8,128)(2,1)} %bitcast.243), calls=%async_computation.2 | async-start | bytes 4194304 | tf_op jit(solution)/shard_map/all_to_all | solution.py:160
  190.4 5.9 %fusion.14 = bf16[1,128,8192]{1,2,0:T(8,128)(2,1)} fusion(bf16[384,128]{1,0:T(8,128)(2,1)S(1)} %copy-done.21, bf16[1,384,8192]{2,1,0:T(8,128)(2,1)} %get-tuple-element.38), kind=kOutput, calls=%fused_computation.28 | convolution fusion | flops 806354944 | bytes 8486912 | tf_op jit(solution)/shard_map/ho,mhc->moc/dot_general | solution.py:102
  196.3 4.2 %copy.48 = bf16[1,128,8192]{2,1,0:T(8,128)(2,1)} copy(bf16[1,128,8192]{1,2,0:T(8,128)(2,1)} %fusion.14) | data formatting | bytes 4194304 | tf_op jit(solution)/shard_map/convert_element_type | solution.py:102
  200.4 3.8 %copy.82 = bf16[16,8,16,512]{3,2,1,0:T(8,128)(2,1)} copy(bf16[16,8,16,512]{3,1,2,0:T(8,128)(2,1)} %bitcast.245) | data formatting | bytes 4194304
  205.5 13.0 %all-to-all-done.2 = bf16[1,32,4,16,512]{4,3,2,0,1:T(8,128)(2,1)S(1)} async-done(((bf16[1,32,4,16,512]{4,3,2,0,1:T(8,128)(2,1)}), bf16[1,32,4,16,512]{4,3,2,0,1:T(8,128)(2,1)S(1)}, u32[]{:S(2)}, u32[]{:S(2)}) %all-to-all-start.2) | async-done | bytes 2097184 | tf_op jit(solution)/shard_map/all_to_all | solution.py:160
  218.5 1.3 copy-done.6
  219.8 6.3 %all-to-all-start.1 = ((bf16[1,32,4,16,512]{4,3,2,0,1:T(8,128)(2,1)}), bf16[1,32,4,16,512]{4,3,2,0,1:T(8,128)(2,1)S(1)}, u32[]{:S(2)}, u32[]{:S(2)}) async-start(bf16[1,32,4,16,512]{4,3,2,0,1:T(8,128)(2,1)} %bitcast.242), calls=%async_computation.1 | async-start | bytes 4194304 | tf_op jit(solution)/shard_map/all_to_all | solution.py:159
  226.7 2.2 convert_bitcast_fusion
  228.9 0.8 copy.55
  229.7 0.7 copy-done.5
  230.5 3.8 %fusion.24 = f32[2,4,256,256]{3,2,1,0:T(8,128)S(1)} fusion(f32[1,2,4,256,512]{4,3,2,1,0:T(8,128)S(1)} %bitcast.238, bf16[1,2,4,256,512]{4,3,2,1,0:T(8,128)(2,1)S(1)} %copy-done.5, f32[256]{0:T(256)S(1)} %copy-done.31, f32[512,128]{0,1:T(8,128)S(1)} %copy-done.13, f32[512,128]{0,1:T(8,128)S(1)} %copy-done.11), kind=kOutput, calls=%fused_computation.40 | convolution fusion | flops 3223584768 | bytes 8913920 | tf_op jit(solution)/shard_map/transpose(jvp(mlfik,jk->mlfij))/dot_general | solution.py:79
  234.3 1.8 fusion.39
  236.5 2.3 fusion.45
  238.8 5.1 %convolution_bitcast_fusion = f32[1,2,4,256,512]{4,3,2,1,0:T(8,128)} fusion(f32[2,4,256,256]{3,2,1,0:T(8,128)S(1)} %fusion.45, f32[512,128]{0,1:T(8,128)S(1)} %copy-done.13, f32[512,128]{0,1:T(8,128)S(1)} %copy-done.11), kind=kOutput, calls=%fused_computation.50 | convolution fusion | flops 3221356544 | bytes 6815744 | tf_op jit(solution)/shard_map/transpose(jvp(mlfij,jk->mlfik))/dot_general | solution.py:64
  243.9 10.0 %all-to-all-done.1 = bf16[1,32,4,16,512]{4,3,2,0,1:T(8,128)(2,1)S(1)} async-done(((bf16[1,32,4,16,512]{4,3,2,0,1:T(8,128)(2,1)}), bf16[1,32,4,16,512]{4,3,2,0,1:T(8,128)(2,1)S(1)}, u32[]{:S(2)}, u32[]{:S(2)}) %all-to-all-start.1) | async-done | bytes 2097184 | tf_op jit(solution)/shard_map/all_to_all | solution.py:159
  255.1 1.7 copy-done.3
  256.7 0.7 copy-done.8
  257.4 3.3 %fusion.26 = f32[1,2,4,256,512]{4,3,2,1,0:T(8,128)} fusion(f32[1,2,4,16,16,512]{5,4,3,2,1,0:T(8,128)S(1)} %copy.51, f32[2,4,256,512]{3,2,1,0:T(8,128)S(1)} %copy-done.3, bf16[1,2,4,256,512]{4,3,2,1,0:T(8,128)(2,1)S(1)} %copy-done.8, f32[2,4]{1,0:T(2,128)S(1)} %copy-done.33), kind=kLoop, calls=%fused_computation.45 | loop fusion | flops 5242880 | bytes 14680096 | tf_op jit(solution)/shard_map/add | solution.py:162
  (98 shorter events, 7.2 us)
Async XLA Ops:
  0.6 109.2 %copy-start = (bf16[384,384]{1,0:T(8,128)(2,1)S(1)}, bf16[384,384]{1,0:T(8,128)(2,1)}, u32[]{:S(2)}) copy-start(bf16[384,384]{1,0:T(8,128)(2,1)} %param.19) | copy-start | bytes 884740
  0.7 11.7 %copy-start.34 = (f32[128]{0:T(128)}, f32[128]{0:T(128)S(1)}, u32[]{:S(2)}) copy-start(f32[128]{0:T(128)S(1)} %fusion.82) | copy-start | bytes 1540
  0.7 11.7 %copy-start.26 = (f32[256]{0:T(256)}, f32[256]{0:T(256)S(1)}, u32[]{:S(2)}) copy-start(f32[256]{0:T(256)S(1)} %add_multiply_fusion) | copy-start | bytes 3076
  0.7 13.9 %copy-start.30 = (f32[256]{0:T(256)}, f32[256]{0:T(256)S(1)}, u32[]{:S(2)}) copy-start(f32[256]{0:T(256)S(1)} %pad_maximum_fusion.6) | copy-start | bytes 3076
  1.4 10.6 %copy-start.28 = (f32[2,4]{1,0:T(2,128)}, f32[2,4]{1,0:T(2,128)S(1)}, u32[]{:S(2)}) copy-start(f32[2,4]{1,0:T(2,128)S(1)} %neg.17) | copy-start | bytes 100
  2.2 9.8 %copy-start.22 = (f32[2,4,128]{2,1,0:T(4,128)}, f32[2,4,128]{2,1,0:T(4,128)S(1)}, u32[]{:S(2)}) copy-start(f32[2,4,128]{2,1,0:T(4,128)S(1)} %get-tuple-element.34) | copy-start | bytes 12292
  2.3 9.8 %copy-start.24 = (f32[2,4,128]{2,1,0:T(4,128)}, f32[2,4,128]{2,1,0:T(4,128)S(1)}, u32[]{:S(2)}) copy-start(f32[2,4,128]{2,1,0:T(4,128)S(1)} %get-tuple-element.35) | copy-start | bytes 12292
  2.4 9.7 %copy-start.17 = (f32[128,128]{1,0:T(8,128)}, f32[128,128]{1,0:T(8,128)S(1)}, u32[]{:S(2)}) copy-start(f32[128,128]{1,0:T(8,128)S(1)} %broadcast_add_fusion) | copy-start | bytes 196612
  3.3 11.4 %copy-start.10 = (f32[512,128]{0,1:T(8,128)}, f32[512,128]{0,1:T(8,128)S(1)}, u32[]{:S(2)}) copy-start(f32[512,128]{0,1:T(8,128)S(1)} %get-tuple-element.32) | copy-start | bytes 786436
  3.3 11.4 %copy-start.12 = (f32[512,128]{0,1:T(8,128)}, f32[512,128]{0,1:T(8,128)S(1)}, u32[]{:S(2)}) copy-start(f32[512,128]{0,1:T(8,128)S(1)} %get-tuple-element.33) | copy-start | bytes 786436
  18.3 2.0 copy-start.2
  20.4 1.6 copy-start.4
  20.4 2.2 copy-start.7
  20.4 2.2 copy-start.32
  99.2 3.7 %copy-start.19 = (bf16[128,384]{1,0:T(8,128)(2,1)S(1)}, bf16[128,384]{1,0:T(8,128)(2,1)}, u32[]{:S(2)}) copy-start(bf16[128,384]{1,0:T(8,128)(2,1)} %param.17) | copy-start | bytes 294916
  99.2 3.7 %copy-start.36 = (f32[384]{0:T(512)S(1)}, f32[384]{0:T(512)}, u32[]{:S(2)}) copy-start(f32[384]{0:T(512)} %param.18) | copy-start | bytes 4612
  101.6 1.6 copy-start.16
  103.2 6.7 %copy-start.37 = (f32[384]{0:T(512)S(1)}, f32[384]{0:T(512)}, u32[]{:S(2)}) copy-start(f32[384]{0:T(512)} %param.20) | copy-start | bytes 4612
  109.8 8.1 %copy-start.38 = (bf16[1,384,8192]{2,1,0:T(8,128)(2,1)}, bf16[1,384,8192]{2,1,0:T(8,128)(2,1)S(1)}, u32[]{:S(2)}) copy-start(bf16[1,384,8192]{2,1,0:T(8,128)(2,1)S(1)} %get-tuple-element.36) | copy-start | bytes 18874372
  109.8 8.1 %copy-start.20 = (bf16[384,128]{1,0:T(8,128)(2,1)S(1)}, bf16[384,128]{1,0:T(8,128)(2,1)}, u32[]{:S(2)}) copy-start(bf16[384,128]{1,0:T(8,128)(2,1)} %param.21) | copy-start | bytes 294916
  124.4 10.8 %copy-start.39 = (bf16[1,384,8192]{2,1,0:T(8,128)(2,1)S(1)}, bf16[1,384,8192]{2,1,0:T(8,128)(2,1)}, u32[]{:S(2)}) copy-start(bf16[1,384,8192]{2,1,0:T(8,128)(2,1)} %copy-done.38) | copy-start | bytes 18874372
  135.2 4.0 %copy-start.14 = (bf16[128,8192,1]{1,0,2:T(8,128)(2,1)S(1)}, bf16[128,8192,1]{1,0,2:T(8,128)(2,1)}, u32[]{:S(2)}) copy-start(bf16[128,8192,1]{1,0,2:T(8,128)(2,1)} %reshape.262) | copy-start | bytes 6291460
  139.2 4.8 %copy-start.9 = (bf16[1,384,8192]{2,1,0:T(8,128)(2,1)S(1)}, bf16[1,384,8192]{2,1,0:T(8,128)(2,1)}, u32[]{:S(2)}) copy-start(bf16[1,384,8192]{2,1,0:T(8,128)(2,1)} %get-tuple-element.38) | copy-start | bytes 18874372
  139.2 5.2 %copy-start.15 = (bf16[128,8192,1]{1,0,2:T(8,128)(2,1)S(1)}, bf16[128,8192,1]{1,0,2:T(8,128)(2,1)}, u32[]{:S(2)}) copy-start(bf16[128,8192,1]{1,0,2:T(8,128)(2,1)} %reshape.264) | copy-start | bytes 6291460
  168.5 17.4 %all-to-all-start.4 = ((f32[8,642,3]{1,2,0:T(4,128)}), f32[8,642,3]{1,2,0:T(4,128)S(1)}, u32[]{:S(2)}, u32[]{:S(2)}) async-start(f32[8,642,3]{1,2,0:T(4,128)} %bitcast.68), calls=%async_computation.4 | async-start | bytes 196608 | tf_op jit(solution)/shard_map/all_to_all | solution.py:34
  183.7 6.6 %copy-start.21 = (bf16[384,128]{1,0:T(8,128)(2,1)S(1)}, bf16[384,128]{1,0:T(8,128)(2,1)}, u32[]{:S(2)}) copy-start(bf16[384,128]{1,0:T(8,128)(2,1)} %param.21) | copy-start | bytes 294916
  185.9 32.6 %all-to-all-start.2 = ((bf16[1,32,4,16,512]{4,3,2,0,1:T(8,128)(2,1)}), bf16[1,32,4,16,512]{4,3,2,0,1:T(8,128)(2,1)S(1)}, u32[]{:S(2)}, u32[]{:S(2)}) async-start(bf16[1,32,4,16,512]{4,3,2,0,1:T(8,128)(2,1)} %bitcast.243), calls=%async_computation.2 | async-start | bytes 4194304 | tf_op jit(solution)/shard_map/all_to_all | solution.py:160
  218.5 1.3 copy-start.6
  219.8 34.1 %all-to-all-start.1 = ((bf16[1,32,4,16,512]{4,3,2,0,1:T(8,128)(2,1)}), bf16[1,32,4,16,512]{4,3,2,0,1:T(8,128)(2,1)S(1)}, u32[]{:S(2)}, u32[]{:S(2)}) async-start(bf16[1,32,4,16,512]{4,3,2,0,1:T(8,128)(2,1)} %bitcast.242), calls=%async_computation.1 | async-start | bytes 4194304 | tf_op jit(solution)/shard_map/all_to_all | solution.py:159
  228.8 1.6 copy-start.5
  228.9 1.6 copy-start.11
  228.9 1.6 copy-start.13
  228.9 1.6 copy-start.31
  230.5 3.8 %copy-start.27 = (f32[256]{0:T(256)S(1)}, f32[256]{0:T(256)}, u32[]{:S(2)}) copy-start(f32[256]{0:T(256)} %copy-done.26) | copy-start | bytes 3076
  230.5 3.8 %copy-start.35 = (f32[128]{0:T(128)S(1)}, f32[128]{0:T(128)}, u32[]{:S(2)}) copy-start(f32[128]{0:T(128)} %copy-done.34) | copy-start | bytes 1540
  230.5 5.6 %copy-start.18 = (f32[128,128]{1,0:T(8,128)S(1)}, f32[128,128]{1,0:T(8,128)}, u32[]{:S(2)}) copy-start(f32[128,128]{1,0:T(8,128)} %copy-done.17) | copy-start | bytes 196612
  230.5 5.7 %copy-start.23 = (f32[2,4,128]{2,1,0:T(4,128)S(1)}, f32[2,4,128]{2,1,0:T(4,128)}, u32[]{:S(2)}) copy-start(f32[2,4,128]{2,1,0:T(4,128)} %copy-done.22) | copy-start | bytes 12292
  230.5 5.7 %copy-start.25 = (f32[2,4,128]{2,1,0:T(4,128)S(1)}, f32[2,4,128]{2,1,0:T(4,128)}, u32[]{:S(2)}) copy-start(f32[2,4,128]{2,1,0:T(4,128)} %copy-done.24) | copy-start | bytes 12292
  230.5 5.7 %copy-start.29 = (f32[2,4]{1,0:T(2,128)S(1)}, f32[2,4]{1,0:T(2,128)}, u32[]{:S(2)}) copy-start(f32[2,4]{1,0:T(2,128)} %copy-done.28) | copy-start | bytes 100
  254.5 2.2 copy-start.3
  254.5 2.9 %copy-start.8 = (bf16[1,2,4,256,512]{4,3,2,1,0:T(8,128)(2,1)S(1)}, bf16[1,2,4,256,512]{4,3,2,1,0:T(8,128)(2,1)}, u32[]{:S(2)}) copy-start(bf16[1,2,4,256,512]{4,3,2,1,0:T(8,128)(2,1)} %param.12) | copy-start | bytes 6291460
  254.6 2.9 %copy-start.33 = (f32[2,4]{1,0:T(2,128)S(1)}, f32[2,4]{1,0:T(2,128)}, u32[]{:S(2)}) copy-start(f32[2,4]{1,0:T(2,128)} %param.16) | copy-start | bytes 100
  254.6 6.1 %copy-start.1 = (bf16[384,384]{1,0:T(8,128)(2,1)S(1)}, bf16[384,384]{1,0:T(8,128)(2,1)}, u32[]{:S(2)}) copy-start(bf16[384,384]{1,0:T(8,128)(2,1)} %param.19) | copy-start | bytes 884740
where the time goes:
time: 265 us; the launch traced here: 261 us
  matrix products  81.7 us (31%)
  blocking collectives  77.8 us (29%)
  local copies, waits for them, and re-layouts  47.8 us (18%)
  waiting for transfers between devices  23 us (9%)
  starting transfers between devices  17.1 us (6%)
  other arithmetic  12 us (5%)
    all_to_all x1, blocking collectives, in_one_piece(): lax.all_to_all(both, axis, split_axis=split_dim, concat_axis=concat_dim,...  56.8 us
    unnamed x85, local copies, waits for them, and re-layouts  21.5 us
    all_to_all x1, blocking collectives, summed_on_arrival(): tiles = lax.all_to_all(cut_along(shard, dim, size), axis, 0, 0, tiled=True)  21 us
    all_to_all x1, waiting for transfers between devices, per_device(): lax.all_to_all(back_cols, 'level', split_axis=1, concat_axis=3, tiled=True)  13 us
    dot_general x2, matrix products, spectral_step(): jnp.einsum('mlfij,jk->mlfik', fields, lon_fwd, precision=highest)  11 us
    dot_general x1, matrix products, columns_backward(): jnp.einsum('ih,mhc->mic', w_mid, slope_two, preferred_element_type=jnp.fl...  10.7 us
    all_to_all x1, waiting for transfers between devices, per_device(): lax.all_to_all(tend_cols, 'level', split_axis=1, concat_axis=3, tiled=True)  10 us
    dot_general x1, matrix products, columns_forward(): jnp.einsum('ih,mic->mhc', w_mid, act_one, preferred_element_type=jnp.floa...  8.11 us
  transfers between devices with their start and end apart: 3, of which 2 were waited for; matrix products, arithmetic and copies ran while one was open for 16% of the time, Pallas kernels for 0%

commit v1 on v0

v1 whole, which is shorter than its diff:
```python
import functools
import math

import jax
import jax.numpy as jnp
import ml_dtypes
import numpy as np
from jax import lax
from jax.experimental import pallas as pl
from jax.experimental.pallas import tpu as pltpu
from jax.sharding import PartitionSpec as P

WAVES = 128
MODES = 128
F32 = jnp.float32
BF16 = jnp.bfloat16
MESH = pl.DeviceIdType.MESH


def halves_np(table):
    high = table.astype(ml_dtypes.bfloat16)
    low = (table - high.astype(np.float64)).astype(ml_dtypes.bfloat16)
    return high, low


def tables(lat_count, lon_count):
    lon = np.arange(lon_count)[:, None] * np.arange(WAVES)[None, :] % lon_count
    phase = 2.0 * np.pi * lon / lon_count
    lon_fwd = np.concatenate([np.cos(phase), np.sin(phase)], axis=1)
    turn = (2 * np.arange(lat_count)[:, None] + 1) * np.arange(MODES)[None, :] % (4 * lat_count)
    lat_fwd = np.cos(np.pi * turn / (2 * lat_count))
    out = []
    for table in (lon_fwd, lon_fwd.T, lat_fwd, lat_fwd.T):
        out.extend(halves_np(np.ascontiguousarray(table)))
    return out


def halves(x):
    high = x.astype(BF16)
    return high, (x - high.astype(F32)).astype(BF16)


def dot(a, b):
    return jnp.dot(a, b, preferred_element_type=F32)


def dot_nt(a, b):
    return lax.dot_general(a, b, (((1,), (1,)), ((), ())), preferred_element_type=F32)


def dot3(a, b):
    return dot(a[0], b[0]) + dot(a[0], b[1]) + dot(a[1], b[0])


def put_rows(ref, rows, x):
    for c in range(x.shape[1] // 128):
        ref[c, rows, :] = x[:, c * 128 : (c + 1) * 128]


def get_rows(ref, rows, first, count):
    return jnp.concatenate([ref[c, rows, :] for c in range(first, first + count)], axis=1)


def sigmoid(x):
    return 0.5 * jnp.tanh(0.5 * x) + 0.5


def kernel(
    levels, members, lat_count, lon_count, hidden,
    shift_ref, visc_ref, ns_ref, state_hbm, noise_hbm, cot_hbm,
    w_in_ref, b_in_ref, w_mid_ref, b_mid_ref, w_out_ref,
    lfh_ref, lfl_ref, lth_ref, ltl_ref, lah_ref, lal_ref, ath_ref, atl_ref,
    next_hbm, grad_hbm, gin_ref, gmid_ref, gout_ref, gbias_ref,
    state_v, noise_v, cot_v, g16, rg, h16, rh, tb, tbr, next_v, z_v, h32, st_v, t_v,
    win_t, wmid_t, wout_t, bb1, bb2, cs_v, sn_v, gi_a, gm_a, go_a, s1_a, s2_a,
    gs, gr, ms, mr,
    in_sem, out_sem, g_send, g_recv, h_send, h_recv, t_send, t_recv, s_send, s_recv, m_send, m_recv,
):
    me = lax.axis_index("level")
    mem = lax.axis_index("member")
    blocks = lat_count // 32
    fields = 8
    waves = 2 * WAVES
    lon_tiles = lon_count // 128
    wave_tiles = waves // 128

    load_noise = pltpu.make_async_copy(noise_hbm, noise_v, in_sem.at[0])
    load_cot = pltpu.make_async_copy(cot_hbm, cot_v, in_sem.at[1])
    load_state = pltpu.make_async_copy(state_hbm, state_v, in_sem.at[2])
    load_noise.start()
    load_cot.start()
    load_state.start()

    barrier = pltpu.get_barrier_semaphore()

    def greet_level(d, _):
        pl.semaphore_signal(
            barrier, inc=1, device_id={"level": lax.rem(me + d, levels)}, device_id_type=MESH
        )
        return 0

    def greet_member(d, _):
        pl.semaphore_signal(
            barrier, inc=1, device_id={"member": lax.rem(mem + d, members)}, device_id_type=MESH
        )
        return 0

    lax.fori_loop(1, levels, greet_level, 0)
    lax.fori_loop(1, members, greet_member, 0)
    pl.semaphore_wait(barrier, levels + members - 2)

    def noise_scale(f):
        return ns_ref[f // 4, f % 4]

    load_noise.wait()
    load_cot.wait()

    def make_grad(a, _):
        rows = pl.ds(pl.multiple_of(a * 32, 32), 32)
        for f in range(fields):
            factor = 1.0 + noise_scale(f) * noise_v[f, rows, :].astype(F32)
            put_rows(st_v, pl.ds(f, 32, stride=fields), cot_v[f, rows, :].astype(F32) * factor)
        g16[a] = get_rows(st_v, slice(None), 0, lon_tiles).astype(BF16).reshape(levels, 16, lon_count)
        return 0

    lax.fori_loop(0, blocks, make_grad, 0)

    def send_grad(d, _):
        to = lax.rem(me + d, levels)
        pltpu.make_async_remote_copy(
            g16.at[:, pl.ds(to, 1)], rg.at[:, pl.ds(me, 1)], g_send, g_recv,
            device_id={"level": to}, device_id_type=MESH,
        ).start()
        return 0

    lax.fori_loop(1, levels, send_grad, 0)
    rg[:, pl.ds(me, 1)] = g16[:, pl.ds(me, 1)]

    field_row = lax.broadcasted_iota(jnp.int32, (fields, WAVES), 0)
    wave = lax.broadcasted_iota(jnp.int32, (fields, WAVES), 1).astype(F32)
    shift = jnp.zeros((fields, WAVES), F32)
    for f in range(fields):
        shift = jnp.where(field_row == f, shift_ref[f // 4, f % 4], shift)
    cs_v[...] = jnp.cos(shift * wave)
    sn_v[...] = jnp.sin(shift * wave)
    p_index = lax.broadcasted_iota(jnp.int32, (MODES, WAVES), 0).astype(F32)
    k_index = lax.broadcasted_iota(jnp.int32, (MODES, WAVES), 1).astype(F32)
    radial = (k_index / WAVES) ** 2 + (p_index / MODES) ** 2
    weight = (
        jnp.where(p_index == 0, 1.0, 2.0) / lat_count * (jnp.where(k_index == 0, 1.0, 2.0) / lon_count)
    )

    def rotation(f):
        damping = jnp.exp(-visc_ref[f // 4, f % 4] * radial) * weight
        return cs_v[pl.ds(f, 1), :] * damping, sn_v[pl.ds(f, 1), :] * damping

    lf = (lfh_ref, lfl_ref)
    lt = (lth_ref, ltl_ref)
    la = (lah_ref, lal_ref)
    at = (ath_ref, atl_ref)

    def both(pair):
        return pair[0][...], pair[1][...]

    load_state.wait()

    def forward(f, _):
        partial = halves(dot3(halves(state_v[f]), both(lf)))
        spectrum = dot3(both(at), partial)
        cosine, sine = rotation(f)
        a, b = spectrum[:, :WAVES], spectrum[:, WAVES:]
        rotated = jnp.concatenate([a * cosine - b * sine, a * sine + b * cosine], axis=1)
        put_rows(h32, pl.ds(f, lat_count, stride=fields), dot3(both(la), halves(rotated)))
        return 0

    lax.fori_loop(0, fields, forward, 0)

    def pack_rows(a, _):
        rows = pl.ds(pl.multiple_of(a * 256, 256), 256)
        h16[a] = get_rows(h32, rows, 0, wave_tiles).astype(BF16).reshape(levels, 16, waves)
        return 0

    lax.fori_loop(0, blocks, pack_rows, 0)

    def send_rows(d, _):
        to = lax.rem(me + d, levels)
        pltpu.make_async_remote_copy(
            h16.at[:, pl.ds(to, 1)], rh.at[:, pl.ds(me, 1)], h_send, h_recv,
            device_id={"level": to}, device_id_type=MESH,
        ).start()
        return 0

    lax.fori_loop(1, levels, send_rows, 0)
    rh[:, pl.ds(me, 1)] = h16[:, pl.ds(me, 1)]

    win_t[...] = w_in_ref[...].astype(F32).T.astype(BF16)
    wmid_t[...] = w_mid_ref[...].astype(F32).T.astype(BF16)
    wout_t[...] = w_out_ref[...].astype(F32).T.astype(BF16)
    bb1[...] = jnp.broadcast_to(b_in_ref[...], (128, hidden)).T
    bb2[...] = jnp.broadcast_to(b_mid_ref[...], (128, hidden)).T
    gi_a[...] = jnp.zeros_like(gi_a)
    gm_a[...] = jnp.zeros_like(gm_a)
    go_a[...] = jnp.zeros_like(go_a)
    s1_a[...] = jnp.zeros_like(s1_a)
    s2_a[...] = jnp.zeros_like(s2_a)

    def local(f, _):
        rows = get_rows(h32, pl.ds(f, lat_count, stride=fields), 0, wave_tiles)
        next_v[f] = dot3(halves(rows), both(lt))
        cot = cot_v[f]
        z_v[f] = dot(cot, lfh_ref[...]) + dot(cot, lfl_ref[...])
        return 0

    lax.fori_loop(0, fields, local, 0)

    others = pl.ds(0, levels - 1)

    def wait_for(ref, sem):
        pltpu.make_async_copy(ref, ref, sem).wait()

    wait_for(rg.at[:, others], g_recv)
    wait_for(rh.at[:, others], h_recv)

    def lanes(x):
        x = x.reshape(levels, 2, 8, lon_count)
        return jnp.concatenate(
            [x[:, r].reshape(levels * 8, lon_count) for r in range(2)], axis=1
        ).astype(BF16)

    def rows_of(x0, x1, width):
        parts = [x.reshape(levels, 8, width) for x in (x0, x1)]
        return jnp.concatenate(parts, axis=1).astype(BF16)

    def lane_sum(x):
        out = x[:, :128]
        for c in range(1, x.shape[1] // 128):
            out = out + x[:, c * 128 : (c + 1) * 128]
        return out

    cols = 2 * lon_count

    def columns(a, _):
        spec = rh[a].reshape(levels * 16, waves)
        inp = lanes(dot(spec, lth_ref[...]) + dot(spec, ltl_ref[...]))
        gt = lanes(rg[a].reshape(levels * 16, lon_count).astype(F32))
        pre = dot(win_t[...], inp) + jnp.tile(bb1[...], (1, cols // 128))
        sg = sigmoid(pre)
        act = pre * sg
        slope1 = sg + act * (1.0 - sg)
        act1 = act.astype(BF16)
        pre = dot(wmid_t[...], act1) + jnp.tile(bb2[...], (1, cols // 128))
        sg = sigmoid(pre)
        act = pre * sg
        slope2 = sg + act * (1.0 - sg)
        act2 = act.astype(BF16)
        tend = dot(wout_t[...], act2)
        tb[a, :, :, pl.ds(0, lon_count)] = rows_of(tend[:, :lon_count], tend[:, lon_count:], lon_count)
        go_a[...] += dot_nt(act2, gt)
        slope = dot(w_out_ref[...], gt) * slope2
        s2_a[...] += lane_sum(slope)
        s2 = slope.astype(BF16)
        gm_a[...] += dot_nt(s2, act1)
        slope = dot(w_mid_ref[...], s2) * slope1
        s1_a[...] += lane_sum(slope)
        s1 = slope.astype(BF16)
        gi_a[...] += dot_nt(s1, inp)
        back = dot(w_in_ref[...], s1).astype(BF16)
        back = jnp.concatenate([back[:, :lon_count], back[:, lon_count:]], axis=0)
        back = dot(back, lfh_ref[...]) + dot(back, lfl_ref[...])
        half = levels * 8
        tb[a, :, :, pl.ds(lon_count, waves)] = rows_of(back[:half], back[half:], waves)

        def send_back(d, _):
            to = lax.rem(me + d, levels)
            pltpu.make_async_remote_copy(
                tb.at[a, pl.ds(to, 1)], tbr.at[a, pl.ds(me, 1)], t_send, t_recv.at[a],
                device_id={"level": to}, device_id_type=MESH,
            ).start()
            return 0

        lax.fori_loop(1, levels, send_back, 0)
        tbr[a, pl.ds(me, 1)] = tb[a, pl.ds(me, 1)]
        return 0

    lax.fori_loop(0, blocks, columns, 0)

    share = hidden // levels
    groups = share // 8
    width = 640

    def column_sum(x):
        return jnp.sum(x, axis=1, keepdims=True)

    lane = lax.broadcasted_iota(jnp.int32, (8, 128), 1)

    def pack_grads(t, _):
        start = t * share
        pieces = []
        bias = jnp.zeros((8, 128), F32)
        for g in range(groups):
            rows = pl.ds(pl.multiple_of(start + 8 * g, 8), 8)
            pieces.append(jnp.concatenate([gi_a[rows, :], gm_a[rows, :], go_a[rows, :]], axis=1))
            bias = jnp.where(lane == 2 * g, column_sum(s1_a[rows, :]), bias)
            bias = jnp.where(lane == 2 * g + 1, column_sum(s2_a[rows, :]), bias)
        top = jnp.concatenate([pieces[0], pieces[2][:, :384]], axis=1)
        low = jnp.concatenate([pieces[1], pieces[2][:, 384:], bias], axis=1)
        gs[t] = jnp.concatenate([top, low], axis=0).astype(BF16)
        return 0

    lax.fori_loop(0, levels, pack_grads, 0)

    def send_grads(d, _):
        to = lax.rem(me + d, levels)
        pltpu.make_async_remote_copy(
            gs.at[pl.ds(to, 1)], gr.at[pl.ds(me, 1)], s_send, s_recv,
            device_id={"level": to}, device_id_type=MESH,
        ).start()
        return 0

    lax.fori_loop(1, levels, send_grads, 0)
    gr[pl.ds(me, 1)] = gs[pl.ds(me, 1)]

    def arrive(a, _):
        wait_for(tbr.at[a, others], t_recv.at[a])
        put_rows(t_v, slice(None), tbr[a].astype(F32).reshape(256, lon_count + waves))
        rows = pl.ds(pl.multiple_of(a * 32, 32), 32)
        for f in range(fields):
            mine = pl.ds(f, 32, stride=fields)
            factor = 1.0 + noise_scale(f) * noise_v[f, rows, :].astype(F32)
            next_v[f, rows, :] += get_rows(t_v, mine, 0, lon_tiles) * factor
            z_v[f, rows, :] += get_rows(t_v, mine, lon_tiles, wave_tiles)
        pltpu.make_async_copy(next_v.at[:, rows], next_hbm.at[:, rows], out_sem.at[0]).start()
        return 0

    lax.fori_loop(0, blocks - 1, arrive, 0)

    wait_for(gr.at[others], s_recv)
    total = gr[0].astype(F32)
    for s in range(1, levels):
        total = total + gr[s].astype(F32)
    ms[...] = total.astype(BF16)

    def send_sums(d, _):
        to = lax.rem(mem + d, members)
        pltpu.make_async_remote_copy(
            ms, mr.at[mem], m_send, m_recv, device_id={"member": to}, device_id_type=MESH
        ).start()
        return 0

    lax.fori_loop(1, members, send_sums, 0)
    mr[mem] = ms[...]

    arrive(blocks - 1, 0)

    def backward(f, _):
        spectrum = dot3(both(at), halves(z_v[f]))
        cosine, sine = rotation(f)
        a, b = spectrum[:, :WAVES], spectrum[:, WAVES:]
        turned = jnp.concatenate([a * cosine + b * sine, b * cosine - a * sine], axis=1)
        rows = halves(dot3(both(la), halves(turned)))
        state_v[f] = dot3(rows, both(lt))
        pltpu.make_async_copy(state_v.at[f], grad_hbm.at[f], out_sem.at[1]).start()
        return 0

    lax.fori_loop(0, fields, backward, 0)

    wait_for(mr.at[pl.ds(0, members - 1)], m_recv)
    total = mr[0].astype(F32)
    for s in range(1, members):
        total = total + mr[s].astype(F32)
    total = total * (1.0 / math.sqrt(members * lat_count * lon_count))
    third = jnp.concatenate([total[:8, width:], total[8:, width : width + 256]], axis=1)
    bias = total[8:, width + 256 :]
    own = share // members
    picked = jnp.concatenate([total[:8, :width], total[8:, :width], third], axis=0)
    unit = lax.broadcasted_iota(jnp.int32, (share, 128), 0)
    slot = lax.broadcasted_iota(jnp.int32, (share, 128), 1)
    choose = jnp.where((unit == mem * own + slot) & (slot < own), 1.0, 0.0)

    def select(block, pick):
        return lax.dot_general(
            block, pick, (((0,), (0,)), ((), ())),
            precision=lax.Precision.HIGHEST, preferred_element_type=F32,
        )

    gin_ref[...] = select(picked[:, :128], choose)[:, :own]
    gmid_ref[...] = select(picked[:, 128:512], choose)[:, :own]
    gout_ref[...] = select(picked[:, 512:640], choose)[:, :own]
    sums = jnp.zeros((128, 128), F32)
    for g in range(groups):
        part = select(bias, choose[8 * g : 8 * g + 8])
        sums = sums + jnp.concatenate([part[2 * g : 2 * g + 2], jnp.zeros((126, 128), F32)], axis=0)
    gbias_ref[...] = sums[:2, :own]

    wait_for(g16.at[:, others], g_send)
    wait_for(h16.at[:, others], h_send)
    wait_for(tb.at[:, others], t_send)
    wait_for(gs.at[others], s_send)
    wait_for(mr.at[pl.ds(0, members - 1)], m_send)
    pltpu.make_async_copy(next_v, next_hbm, out_sem.at[0]).wait()
    pltpu.make_async_copy(state_v, grad_hbm, out_sem.at[1]).wait()


def per_device(levels, members, state, noise, cot, shift, visc, ns, w_in, b_in, w_mid, b_mid, w_out):
    shape = state.shape
    lat_count, lon_count = shape[3:]
    fields = shape[0] * shape[1] * shape[2]
    hidden = w_in.shape[1]
    blocks = lat_count // 32
    waves = 2 * WAVES
    flat = (fields, lat_count, lon_count)
    own = hidden // levels // members
    smem = pl.BlockSpec(memory_space=pltpu.SMEM)
    hbm = pl.BlockSpec(memory_space=pl.ANY)
    vmem = pl.BlockSpec(memory_space=pltpu.VMEM)
    dma = pltpu.SemaphoreType.DMA
    out = pl.pallas_call(
        functools.partial(kernel, levels, members, lat_count, lon_count, hidden),
        name="ensemble_step",
        out_shape=(
            jax.ShapeDtypeStruct(flat, F32),
            jax.ShapeDtypeStruct(flat, F32),
            jax.ShapeDtypeStruct((w_in.shape[0], own), F32),
            jax.ShapeDtypeStruct((hidden, own), F32),
            jax.ShapeDtypeStruct((w_out.shape[1], own), F32),
            jax.ShapeDtypeStruct((2, own), F32),
        ),
        in_specs=[smem] * 3 + [hbm] * 3 + [vmem] * 13,
        out_specs=(hbm, hbm, vmem, vmem, vmem, vmem),
        scratch_shapes=[
            pltpu.VMEM(flat, F32),
            pltpu.VMEM(flat, BF16),
            pltpu.VMEM(flat, BF16),
            pltpu.VMEM((blocks, levels, 16, lon_count), BF16),
            pltpu.VMEM((blocks, levels, 16, lon_count), BF16),
            pltpu.VMEM((blocks, levels, 16, waves), BF16),
            pltpu.VMEM((blocks, levels, 16, waves), BF16),
            pltpu.VMEM((blocks, levels, 16, lon_count + waves), BF16),
            pltpu.VMEM((blocks, levels, 16, lon_count + waves), BF16),
            pltpu.VMEM(flat, F32),
            pltpu.VMEM((fields, lat_count, waves), F32),
            pltpu.VMEM((waves // 128, lat_count * fields, 128), F32),
            pltpu.VMEM((lon_count // 128, 256, 128), F32),
            pltpu.VMEM(((lon_count + waves) // 128, 256, 128), F32),
            pltpu.VMEM((hidden, w_in.shape[0]), BF16),
            pltpu.VMEM((hidden, hidden), BF16),
            pltpu.VMEM((w_out.shape[1], hidden), BF16),
            pltpu.VMEM((hidden, 128), F32),
            pltpu.VMEM((hidden, 128), F32),
            pltpu.VMEM((fields, WAVES), F32),
            pltpu.VMEM((fields, WAVES), F32),
            pltpu.VMEM((hidden, 128), F32),
            pltpu.VMEM((hidden, hidden), F32),
            pltpu.VMEM((hidden, 128), F32),
            pltpu.VMEM((hidden, 128), F32),
            pltpu.VMEM((hidden, 128), F32),
            pltpu.VMEM((levels, 16, 1024), BF16),
            pltpu.VMEM((levels, 16, 1024), BF16),
            pltpu.VMEM((16, 1024), BF16),
            pltpu.VMEM((members, 16, 1024), BF16),
            dma((3,)),
            dma((2,)),
            dma(()),
            dma(()),
            dma(()),
            dma(()),
            dma(()),
            dma((blocks,)),
            dma(()),
            dma(()),
            dma(()),
            dma(()),
        ],
        compiler_params=pltpu.CompilerParams(
            collective_id=0, has_side_effects=True, vmem_limit_bytes=60 << 20
        ),
    )(
        shift, visc, ns, state.reshape(flat), noise.reshape(flat), cot.reshape(flat),
        w_in, b_in.reshape(1, -1), w_mid, b_mid.reshape(1, -1), w_out,
        *[jnp.asarray(t) for t in tables(lat_count, lon_count)],
    )
    return (out[0].reshape(shape), out[1].reshape(shape), *out[2:])


def solution(mesh):
    grid = P("member", "level", None, None, None)
    return jax.shard_map(
        functools.partial(per_device, mesh.shape["level"], mesh.shape["member"]),
        mesh=mesh,
        in_specs=(grid, grid, grid, P("level", None), P("level", None), P("level", None))
        + (P(),) * 5,
        out_specs=(grid, grid) + (P(None, ("level", "member")),) * 4,
        check_vma=False,
    )
```

time: 265 us -> 124 us (0.47); the launches traced: 261 us -> 123 us
  Pallas kernels: 0 us -> 108 us
  matrix products: 81.7 us -> 0 us
  blocking collectives: 77.8 us -> 0 us
  local copies, waits for them, and re-layouts: 47.8 us -> 14.5 us
  waiting for transfers between devices: 23 us -> 0 us
  starting transfers between devices: 17.1 us -> 0 us
  other arithmetic: 12 us -> 0 us
    pallas_call x0 -> x1, Pallas kernels: none -> 108 us  [per_device(): pl.pallas_call(functools.partial(kernel, levels, members, lat_count, lon_...]
    dot_general x17 -> x0, matrix products: 81.7 us -> none  [the longest x2 11 us: spectral_step(): jnp.einsum('mlfij,jk->mlfik', fields, lon_fwd, precision=highest)]
    all_to_all x2 -> x0, blocking collectives: 77.8 us -> none  [the longest x1 56.8 us: in_one_piece(): lax.all_to_all(both, axis, split_axis=split_dim, concat_axis=concat_dim,...]
    all_to_all x3 -> x0, waiting for transfers between devices: 23 us -> none  [the longest x1 13 us: per_device(): lax.all_to_all(back_cols, 'level', split_axis=1, concat_axis=3, tiled=True)]
    all_to_all x3 -> x0, starting transfers between devices: 17.1 us -> none  [the longest x1 6.35 us: summed_on_arrival(): tiles = lax.all_to_all(cut_along(shard, dim, size), axis, 0, 0, tiled=True)]
    unnamed x85 -> x10, local copies, waits for them, and re-layouts: 21.5 us -> 12 us
    convert_element_type x4 -> x0, local copies, waits for them, and re-layouts: 8.34 us -> none  [the longest x1 4.15 us: columns_forward(): jnp.einsum('ho,mhc->moc', w_out, act_two, preferred_element_type=jnp.floa...]
    another operation x2 -> x0, local copies, waits for them, and re-layouts: 6.55 us -> none
  transfers between devices with their start and end apart: 3 -> 0, of which waited for: 2 -> 0; matrix products, arithmetic and copies ran while one was open for 16% -> 0% of each run, Pallas kernels for 0% -> 0%
where the time goes in v1:
time: 124 us; the launch traced here: 123 us
  Pallas kernels  108 us (87%)
  local copies, waits for them, and re-layouts  14.5 us (12%)
    pallas_call x1, Pallas kernels, per_device(): pl.pallas_call(functools.partial(kernel, levels, members, lat_count, lon_...  108 us
    unnamed x10, local copies, waits for them, and re-layouts  12 us

profile of v1, /device:TPU:1, one launch (start us, length us, event | category | flops | bytes accessed | tf_op | source)
XLA Modules:
  0.0 123.2 jit_solution(6198777271032726079)
XLA Ops:
  0.6 1.2 %reshape.36.b_in_ref = f32[1,384]{1,0:T(1,128)} reshape(f32[384]{0:T(512)} %param.26) | data formatting | bytes 3072 | tf_op jit(solution)/shard_map/reshape | solution.py:479
  1.9 1.2 %reshape.37.b_mid_ref = f32[1,384]{1,0:T(1,128)} reshape(f32[384]{0:T(512)} %param.28) | data formatting | bytes 3072 | tf_op jit(solution)/shard_map/reshape | solution.py:479
  3.1 108.1 %ensemble_step.1 = (f32[8,256,512]{2,1,0:T(8,128)}, f32[8,256,512]{2,1,0:T(8,128)}, f32[128,3]{1,0:T(8,128)}, f32[384,3]{1,0:T(8,128)}, f32[128,3]{1,0:T(8,128)}, /*index=5*/f32[2,3]{1,0:T(2,128)}) custom-call(f32[2,4]{1,0:T(2,128)} %shift_ref.1, f32[2,4]{1,0:T(2,128)} %visc_ref.1, f32[2,4]{1,0:T(2,128)} %ns_ref.1, f32[8,256,512]{2,1,0:T(8,128)} %bitcast.5, ...), custom_call_target="tpu_custom_call" | custom-call | tf_op jit(solution)/shard_map/ensemble_step/pallas_call | solution.py:417
  111.2 1.5 %copy.25 = f32[128,3]{0,1:T(4,128)} copy(f32[128,3]{1,0:T(8,128)} %get-tuple-element.20) | data formatting | bytes 3072
  112.7 1.5 %copy.27 = f32[128,3]{0,1:T(4,128)} copy(f32[128,3]{1,0:T(8,128)} %get-tuple-element.22) | data formatting | bytes 3072
  114.2 1.6 %copy.26 = f32[384,3]{0,1:T(4,128)} copy(f32[384,3]{1,0:T(8,128)} %get-tuple-element.21) | data formatting | bytes 9216
  115.8 0.0 copy-start
  115.8 4.8 %copy.31 = f32[1,2,4,256,512]{4,3,2,1,0:T(8,128)} copy(f32[1,2,4,256,512]{4,3,2,1,0:T(8,128)} %bitcast.7) | data formatting | bytes 8388608
  120.6 0.0 copy-done
  120.6 0.0 copy-start.1
  120.6 2.0 %copy.32 = f32[1,2,4,256,512]{4,3,2,1,0:T(8,128)} copy(f32[1,2,4,256,512]{4,3,2,1,0:T(8,128)S(1)} %bitcast.6) | data formatting | bytes 8388608
  122.6 0.0 copy-done.1
  122.6 0.6 copy.33
Async XLA Ops:
  115.8 4.8 %copy-start = (f32[8,256,512]{2,1,0:T(8,128)S(1)}, f32[8,256,512]{2,1,0:T(8,128)}, u32[]{:S(2)}) copy-start(f32[8,256,512]{2,1,0:T(8,128)} %get-tuple-element.13) | copy-start | bytes 12582916
  120.6 2.0 %copy-start.1 = (f32[2,3]{1,0:T(2,128)S(1)}, f32[2,3]{1,0:T(2,128)}, u32[]{:S(2)}) copy-start(f32[2,3]{1,0:T(2,128)} %get-tuple-element.35) | copy-start | bytes 76

commit v2 on v1

v2 whole, which is shorter than its diff:
```python
import functools
import math

import jax
import jax.numpy as jnp
import ml_dtypes
import numpy as np
from jax import lax
from jax.experimental import pallas as pl
from jax.experimental.pallas import tpu as pltpu
from jax.sharding import PartitionSpec as P

WAVES = 128
MODES = 128
F32 = jnp.float32
BF16 = jnp.bfloat16
MESH = pl.DeviceIdType.MESH
EARLY = 3
VMEM_LIMIT = 46 << 20


def halves_np(table):
    high = table.astype(ml_dtypes.bfloat16)
    low = (table - high.astype(np.float64)).astype(ml_dtypes.bfloat16)
    return high, low


def tables(lat_count, lon_count):
    lon = np.arange(lon_count)[:, None] * np.arange(WAVES)[None, :] % lon_count
    phase = 2.0 * np.pi * lon / lon_count
    lon_fwd = np.concatenate([np.cos(phase), np.sin(phase)], axis=1)
    turn = (2 * np.arange(lat_count)[:, None] + 1) * np.arange(MODES)[None, :] % (4 * lat_count)
    lat_fwd = np.cos(np.pi * turn / (2 * lat_count))
    out = []
    for table in (lon_fwd, lon_fwd.T, lat_fwd, lat_fwd.T):
        out.extend(halves_np(np.ascontiguousarray(table)))
    return out


def unit_order(hidden, levels, members):
    columns = members // 2
    units = np.arange(hidden).reshape(levels, 2, columns, -1)
    order = units.transpose(2, 0, 1, 3).reshape(-1)
    return (order[:, None] == np.arange(hidden)[None, :]).astype(ml_dtypes.bfloat16)


def halves(x):
    high = x.astype(BF16)
    return high, (x - high.astype(F32)).astype(BF16)


def dot(a, b):
    return jnp.dot(a, b, preferred_element_type=F32)


def dot_nt(a, b):
    return lax.dot_general(a, b, (((1,), (1,)), ((), ())), preferred_element_type=F32)


def dot3(a, b):
    return dot(a[0], b[0]) + dot(a[0], b[1]) + dot(a[1], b[0])


def put_rows(ref, rows, x):
    for c in range(x.shape[1] // 128):
        ref[c, rows, :] = x[:, c * 128 : (c + 1) * 128]


def get_rows(ref, rows, first, count):
    return jnp.concatenate([ref[c, rows, :] for c in range(first, first + count)], axis=1)


def sigmoid(x):
    return 0.5 * jnp.tanh(0.5 * x) + 0.5


def kernel(
    levels, members, lat_count, lon_count, hidden,
    shift_ref, visc_ref, ns_ref, state_hbm, noise_hbm, cot_hbm,
    w_in_hbm, w_mid_hbm, w_out_hbm, lfh_hbm, lfl_hbm, lth_hbm, ltl_hbm, lah_hbm, lal_hbm, ath_hbm, atl_hbm,
    order_hbm, b_in_hbm, b_mid_hbm,
    next_v, grad_v, sums_ref,
    w_in_v, w_mid_v, w_out_v, lfh_ref, lfl_ref, lth_ref, ltl_ref, lah_ref, lal_ref, ath_ref, atl_ref,
    order_ref, b_in_ref, b_mid_ref,
    w_in_ref, w_mid_ref, w_out_ref,
    state_v, noise_v, cot_v, g16, rg, h16, rh, tb, tbr, bb, bbr, z_v, h32, st_v, t_v, b_v,
    win_t, wmid_t, wout_t, bb1, bb2, cs_v, sn_v, gi_a, gm_a, go_a, s1_a, s2_a,
    gs, gx, gl, gr, ms, mr,
    in_sem, state_sem, w_sem, g_send, g_recv, h_send, h_recv, t_send, t_recv, b_send, b_recv,
    x_send, x_recv, s_send, s_recv, m_send, m_recv,
):
    me = lax.axis_index("level")
    mem = lax.axis_index("member")
    blocks = lat_count // 32
    fields = 8
    waves = 2 * WAVES
    lon_tiles = lon_count // 128
    wave_tiles = waves // 128

    def load_block(a):
        rows = pl.ds(pl.multiple_of(a * 32, 32), 32)
        return (
            pltpu.make_async_copy(noise_hbm.at[:, rows], noise_v.at[:, rows], in_sem.at[0, a]),
            pltpu.make_async_copy(cot_hbm.at[:, rows], cot_v.at[:, rows], in_sem.at[1, a]),
        )

    for a in range(blocks):
        for copy in load_block(a):
            copy.start()
    load_state = pltpu.make_async_copy(state_hbm, state_v, state_sem)
    load_state.start()
    given = [
        pltpu.make_async_copy(src, dst, w_sem.at[i])
        for i, (src, dst) in enumerate(
            [
                (lfh_hbm, lfh_ref), (lfl_hbm, lfl_ref), (ath_hbm, ath_ref), (atl_hbm, atl_ref),
                (lah_hbm, lah_ref), (lal_hbm, lal_ref), (lth_hbm, lth_ref), (ltl_hbm, ltl_ref),
                (w_in_hbm, w_in_v), (w_mid_hbm, w_mid_v), (w_out_hbm, w_out_v), (order_hbm, order_ref),
                (b_in_hbm, b_in_ref), (b_mid_hbm, b_mid_ref),
            ]
        )
    ]
    for copy in given:
        copy.start()

    barrier = pltpu.get_barrier_semaphore()

    def greet_level(d, _):
        pl.semaphore_signal(
            barrier, inc=1, device_id={"level": lax.rem(me + d, levels)}, device_id_type=MESH
        )
        return 0

    columns_x = members // 2
    my_y, my_x = mem // columns_x, lax.rem(mem, columns_x)
    beside = [my_y * columns_x + lax.rem(my_x + d, columns_x) for d in range(1, columns_x)]
    across = (1 - my_y) * columns_x + my_x

    lax.fori_loop(1, levels, greet_level, 0)
    for to in (*beside, across):
        pl.semaphore_signal(barrier, inc=1, device_id={"member": to}, device_id_type=MESH)
    pl.semaphore_wait(barrier, levels - 1 + columns_x)

    def send_level(src, dst, send, recv):
        def one(d, _):
            to = lax.rem(me + d, levels)
            pltpu.make_async_remote_copy(
                src(to), dst, send, recv, device_id={"level": to}, device_id_type=MESH
            ).start()
            return 0

        lax.fori_loop(1, levels, one, 0)

    mine = pl.ds(me, 1)

    def noise_scale(f):
        return ns_ref[f // 4, f % 4]

    def make_grad(a, _):
        for copy in load_block(a):
            copy.wait()
        rows = pl.ds(pl.multiple_of(a * 32, 32), 32)
        for f in range(fields):
            factor = 1.0 + noise_scale(f) * noise_v[f, rows, :].astype(F32)
            put_rows(st_v, pl.ds(f, 32, stride=fields), cot_v[f, rows, :].astype(F32) * factor)
        g16[a] = get_rows(st_v, slice(None), 0, lon_tiles).astype(BF16).reshape(levels, 16, lon_count)
        send_level(lambda to: g16.at[a, pl.ds(to, 1)], rg.at[a, mine], g_send, g_recv.at[a])
        rg[a, mine] = g16[a, mine]
        return 0

    lax.fori_loop(0, blocks, make_grad, 0)

    field_row = lax.broadcasted_iota(jnp.int32, (fields, WAVES), 0)
    wave = lax.broadcasted_iota(jnp.int32, (fields, WAVES), 1).astype(F32)
    shift = jnp.zeros((fields, WAVES), F32)
    for f in range(fields):
        shift = jnp.where(field_row == f, shift_ref[f // 4, f % 4], shift)
    cs_v[...] = jnp.cos(shift * wave)
    sn_v[...] = jnp.sin(shift * wave)
    p_index = lax.broadcasted_iota(jnp.int32, (MODES, WAVES), 0).astype(F32)
    k_index = lax.broadcasted_iota(jnp.int32, (MODES, WAVES), 1).astype(F32)
    radial = (k_index / WAVES) ** 2 + (p_index / MODES) ** 2
    weight = (
        jnp.where(p_index == 0, 1.0, 2.0) / lat_count * (jnp.where(k_index == 0, 1.0, 2.0) / lon_count)
    )

    def rotation(f):
        damping = jnp.exp(-visc_ref[f // 4, f % 4] * radial) * weight
        return cs_v[pl.ds(f, 1), :] * damping, sn_v[pl.ds(f, 1), :] * damping

    lf = (lfh_ref, lfl_ref)
    lt = (lth_ref, ltl_ref)
    la = (lah_ref, lal_ref)
    at = (ath_ref, atl_ref)

    def both(pair):
        return pair[0][...], pair[1][...]

    load_state.wait()
    for copy in given[:6]:
        copy.wait()

    def forward(f, _):
        partial = halves(dot3(halves(state_v[f]), both(lf)))
        spectrum = dot3(both(at), partial)
        cosine, sine = rotation(f)
        a, b = spectrum[:, :WAVES], spectrum[:, WAVES:]
        rotated = jnp.concatenate([a * cosine - b * sine, a * sine + b * cosine], axis=1)
        put_rows(h32, pl.ds(f, lat_count, stride=fields), dot3(both(la), halves(rotated)))
        return 0

    lax.fori_loop(0, fields, forward, 0)

    def pack_rows(b, _):
        for r in range(2):
            rows = pl.ds(pl.multiple_of(b * 512, 512) + 256 * r, 256)
            packed = get_rows(h32, rows, 0, wave_tiles).astype(BF16)
            h16[2 * b + r] = packed.reshape(levels, 16, waves)
        two = pl.ds(2 * b, 2)
        send_level(lambda to: h16.at[two, pl.ds(to, 1)], rh.at[two, mine], h_send, h_recv.at[b])
        rh[two, mine] = h16[two, mine]
        return 0

    lax.fori_loop(0, blocks // 2, pack_rows, 0)

    for copy in given[6:]:
        copy.wait()

    order = order_ref[...]

    def units_first(bias_ref):
        bias = jnp.broadcast_to(bias_ref[...].reshape(1, hidden), (128, hidden)).T
        high, rest = halves(bias)
        mid, low = halves(bias - high.astype(F32))
        return dot(order, high) + dot(order, mid) + dot(order, low)

    win_t[...] = dot_nt(order, w_in_v[...]).astype(BF16)
    w_in_ref[...] = dot_nt(w_in_v[...], order).astype(BF16)
    w_mid_ref[...] = dot_nt(dot(order, w_mid_v[...]).astype(BF16), order).astype(BF16)
    wmid_t[...] = dot_nt(dot_nt(order, w_mid_v[...]).astype(BF16), order).astype(BF16)
    w_out = dot(order, w_out_v[...])
    w_out_ref[...] = w_out.astype(BF16)
    wout_t[...] = w_out.T.astype(BF16)
    bb1[...] = units_first(b_in_ref)
    bb2[...] = units_first(b_mid_ref)
    gi_a[...] = jnp.zeros_like(gi_a)
    gm_a[...] = jnp.zeros_like(gm_a)
    go_a[...] = jnp.zeros_like(go_a)
    s1_a[...] = jnp.zeros_like(s1_a)
    s2_a[...] = jnp.zeros_like(s2_a)

    def local(f, _):
        rows = get_rows(h32, pl.ds(f, lat_count, stride=fields), 0, wave_tiles)
        next_v[f] = dot3(halves(rows), both(lt))
        cot = cot_v[f]
        z_v[f] = dot(cot, lfh_ref[...]) + dot(cot, lfl_ref[...])
        return 0

    lax.fori_loop(0, fields, local, 0)

    others = pl.ds(0, levels - 1)

    def wait_for(ref, sem):
        pltpu.make_async_copy(ref, ref, sem).wait()


    def lanes(x):
        x = x.reshape(levels, 2, 8, lon_count)
        return jnp.concatenate(
            [x[:, r].reshape(levels * 8, lon_count) for r in range(2)], axis=1
        ).astype(BF16)

    def rows_of(x0, x1, width):
        parts = [x.reshape(levels, 8, width) for x in (x0, x1)]
        return jnp.concatenate(parts, axis=1).astype(BF16)

    def lane_sum(x):
        out = x[:, :128]
        for c in range(1, x.shape[1] // 128):
            out = out + x[:, c * 128 : (c + 1) * 128]
        return out

    cols = 2 * lon_count

    def columns(a, _):
        wait_for(rg.at[a, others], g_recv.at[a])

        @pl.when(lax.rem(a, 2) == 0)
        def _():
            wait_for(rh.at[pl.ds(a, 2), others], h_recv.at[a // 2])

        spec = rh[a].reshape(levels * 16, waves)
        inp = lanes(dot(spec, lth_ref[...]) + dot(spec, ltl_ref[...]))
        gt = lanes(rg[a].reshape(levels * 16, lon_count).astype(F32))
        pre = dot(win_t[...], inp) + jnp.tile(bb1[...], (1, cols // 128))
        sg = sigmoid(pre)
        act = pre * sg
        slope1 = sg + act * (1.0 - sg)
        act1 = act.astype(BF16)
        pre = dot(wmid_t[...], act1) + jnp.tile(bb2[...], (1, cols // 128))
        sg = sigmoid(pre)
        act = pre * sg
        slope2 = sg + act * (1.0 - sg)
        act2 = act.astype(BF16)
        tend = dot(wout_t[...], act2)
        tb[a] = rows_of(tend[:, :lon_count], tend[:, lon_count:], lon_count)
        go_a[...] += dot_nt(act2, gt)
        slope = dot(w_out_ref[...], gt) * slope2
        s2_a[...] += lane_sum(slope)
        s2 = slope.astype(BF16)
        gm_a[...] += dot_nt(s2, act1)
        slope = dot(w_mid_ref[...], s2) * slope1
        s1_a[...] += lane_sum(slope)
        s1 = slope.astype(BF16)
        gi_a[...] += dot_nt(s1, inp)
        back = dot(w_in_ref[...], s1).astype(BF16)
        back = jnp.concatenate([back[:, :lon_count], back[:, lon_count:]], axis=0)
        back = dot(back, lfh_ref[...]) + dot(back, lfl_ref[...])
        half = levels * 8
        bb[a] = rows_of(back[:half], back[half:], waves)

        @pl.when(lax.rem(a, 2) == 1)
        def _():
            two = pl.ds(a - 1, 2)
            send_level(lambda to: bb.at[two, pl.ds(to, 1)], bbr.at[two, mine], b_send, b_recv)
            bbr[two, mine] = bb[two, mine]

        @pl.when(a < EARLY)
        def _():
            send_tend(a, 0)

        return 0

    def send_tend(a, _):
        send_level(lambda to: tb.at[a, pl.ds(to, 1)], tbr.at[a, mine], t_send, t_recv.at[a])
        tbr[a, mine] = tb[a, mine]
        return 0

    lax.fori_loop(0, blocks, columns, 0)

    lane = lax.broadcasted_iota(jnp.int32, (hidden, 128), 1)
    bias = jnp.where(lane == 0, jnp.sum(s1_a[...], axis=1, keepdims=True), 0.0)
    bias = jnp.where(lane == 1, jnp.sum(s2_a[...], axis=1, keepdims=True), bias)
    parts = [gi_a[...].astype(BF16), dot(gm_a[...].astype(BF16), order).astype(BF16)]
    parts += [go_a[...].astype(BF16), bias.astype(BF16)]
    gs[...] = jnp.concatenate(parts, axis=1).reshape(columns_x, hidden // columns_x, 768)
    for d, to in enumerate(beside):
        pltpu.make_async_remote_copy(
            gs.at[lax.rem(my_x + d + 1, columns_x)], gx.at[my_x], x_send, x_recv,
            device_id={"member": to}, device_id_type=MESH,
        ).start()
    gx[my_x] = gs[my_x]
    lax.fori_loop(EARLY, EARLY + 2, send_tend, 0)

    wait_for(bbr.at[:, others], b_recv)

    def gather(a, _):
        put_rows(b_v, slice(None), bbr[a].astype(F32).reshape(256, waves))
        rows = pl.ds(pl.multiple_of(a * 32, 32), 32)
        for f in range(fields):
            z_v[f, rows, :] += get_rows(b_v, pl.ds(f, 32, stride=fields), 0, wave_tiles)
        return 0

    lax.fori_loop(0, blocks, gather, 0)

    def backward(f, _):
        spectrum = dot3(both(at), halves(z_v[f]))
        cosine, sine = rotation(f)
        a, b = spectrum[:, :WAVES], spectrum[:, WAVES:]
        turned = jnp.concatenate([a * cosine + b * sine, b * cosine - a * sine], axis=1)
        rows = halves(dot3(both(la), halves(turned)))
        grad_v[f] = dot3(rows, both(lt))
        late = EARLY + 2 + f // 2

        @pl.when((lax.rem(f, 2) == 0) & (late < blocks))
        def _():
            send_tend(late, 0)

        return 0

    lax.fori_loop(0, fields, backward, 0)

    wait_for(gx.at[pl.ds(0, columns_x - 1)], x_recv)
    total = gx[0].astype(F32)
    for s in range(1, columns_x):
        total = total + gx[s].astype(F32)
    total = total.astype(BF16)
    share = hidden // columns_x // levels
    place = lax.broadcasted_iota(jnp.int32, (levels * 8, hidden // columns_x), 0)
    unit = lax.broadcasted_iota(jnp.int32, (levels * 8, hidden // columns_x), 1)
    within = place & 7
    spread = jnp.where((unit == (place >> 3) * share + within) & (within < share), 1.0, 0.0).astype(BF16)
    pair = [dot(spread, total[:, c : c + 384]).reshape(levels, 8, 384) for c in (0, 384)]
    gl[...] = jnp.concatenate(pair, axis=1).astype(BF16)
    send_level(lambda to: gl.at[pl.ds(to, 1)], gr.at[mine], s_send, s_recv)
    gr[mine] = gl[mine]

    def arrive(a, _):
        wait_for(tbr.at[a, others], t_recv.at[a])
        put_rows(t_v, slice(None), tbr[a].astype(F32).reshape(256, lon_count))
        rows = pl.ds(pl.multiple_of(a * 32, 32), 32)
        for f in range(fields):
            factor = 1.0 + noise_scale(f) * noise_v[f, rows, :].astype(F32)
            next_v[f, rows, :] += get_rows(t_v, pl.ds(f, 32, stride=fields), 0, lon_tiles) * factor
        return 0

    lax.fori_loop(0, blocks - 3, arrive, 0)

    wait_for(gr.at[others], s_recv)
    total = gr[0].astype(F32)
    for s in range(1, levels):
        total = total + gr[s].astype(F32)
    ms[...] = total.astype(BF16)
    swap = pltpu.make_async_remote_copy(
        ms, mr, m_send, m_recv, device_id={"member": across}, device_id_type=MESH
    )
    swap.start()

    lax.fori_loop(blocks - 3, blocks, arrive, 0)

    swap.wait()
    norm = 1.0 / math.sqrt(members * lat_count * lon_count)
    sums_ref[...] = (total + mr[...].astype(F32)) * norm

    wait_for(g16.at[:, others], g_send)
    wait_for(h16.at[:, others], h_send)
    wait_for(tb.at[:, others], t_send)
    wait_for(bb.at[:, others], b_send)
    wait_for(gs.at[pl.ds(0, columns_x - 1)], x_send)
    wait_for(gl.at[others], s_send)


def finish(
    hidden, levels, members, next_in, grad_in, sums_ref, next_out, grad_out, gin_ref, gmid_ref,
    gout_ref, gbias_ref, sem,
):
    stores = []
    for i, (src, dst) in enumerate(((next_in, next_out), (grad_in, grad_out))):
        for f in range(src.shape[0]):
            stores.append(pltpu.make_async_copy(src.at[f], dst.at[f], sem.at[i, f]))
    for store in stores:
        store.start()
    own = hidden // levels // members
    first = lax.axis_index("member") // (members // 2) * own
    slot = lax.broadcasted_iota(jnp.int32, (8, 8), 0)
    unit = lax.broadcasted_iota(jnp.int32, (8, 8), 1)
    choose = jnp.where((unit == first + slot) & (slot < own), 1.0, 0.0)

    def exact(a, b, dims):
        return lax.dot_general(
            a, b, (dims, ((), ())), precision=lax.Precision.HIGHEST, preferred_element_type=F32
        )

    top = exact(choose, sums_ref[:8, :], ((1,), (0,)))
    low = exact(choose, sums_ref[8:, :], ((1,), (0,)))
    gin_ref[...] = top[:own, :128]
    gmid_ref[...] = jnp.concatenate([top[:, 128:], low[:, :128]], axis=1)[:own]
    gout_ref[...] = low[:own, 128:256]
    lane = lax.broadcasted_iota(jnp.int32, (8, 128), 1)
    row = lax.broadcasted_iota(jnp.int32, (8, 128), 0)
    take = jnp.where((lane == row) & (row < 2), 1.0, 0.0)
    gbias_ref[...] = exact(take, low[:, 256:], ((1,), (1,)))[:2, :own]
    for store in stores:
        store.wait()


def per_device(levels, members, state, noise, cot, shift, visc, ns, w_in, b_in, w_mid, b_mid, w_out):
    shape = state.shape
    lat_count, lon_count = shape[3:]
    fields = shape[0] * shape[1] * shape[2]
    hidden = w_in.shape[1]
    blocks = lat_count // 32
    waves = 2 * WAVES
    flat = (fields, lat_count, lon_count)
    own = hidden // levels // members
    smem = pl.BlockSpec(memory_space=pltpu.SMEM)
    hbm = pl.BlockSpec(memory_space=pl.ANY)
    vmem = pl.BlockSpec(memory_space=pltpu.VMEM)
    dma = pltpu.SemaphoreType.DMA
    given = [w_in, w_mid, w_out, *[jnp.asarray(t) for t in tables(lat_count, lon_count)]]
    given += [jnp.asarray(unit_order(hidden, levels, members)), b_in, b_mid]
    grid_rows = pltpu.VMEM((blocks, levels, 16, lon_count), BF16)
    wave_rows = pltpu.VMEM((blocks, levels, 16, waves), BF16)
    per_unit = pltpu.VMEM((hidden, 128), F32)
    state_out, grad_out, sums = pl.pallas_call(
        functools.partial(kernel, levels, members, lat_count, lon_count, hidden),
        name="ensemble_step",
        out_shape=(
            pltpu.VMEM(flat, F32),
            pltpu.VMEM(flat, F32),
            pltpu.VMEM((16, 384), F32),
        ),
        in_specs=[smem] * 3 + [hbm] * (3 + len(given)),
        out_specs=(vmem, vmem, vmem),
        scratch_shapes=[pltpu.VMEM(x.shape, x.dtype) for x in given]
        + [pltpu.VMEM(x.shape, BF16) for x in given[:3]]
        + [
            pltpu.VMEM(flat, F32),
            pltpu.VMEM(flat, BF16),
            pltpu.VMEM(flat, BF16),
            grid_rows, grid_rows, wave_rows, wave_rows, grid_rows, grid_rows, wave_rows, wave_rows,
            pltpu.VMEM((fields, lat_count, waves), F32),
            pltpu.VMEM((waves // 128, lat_count * fields, 128), F32),
            pltpu.VMEM((lon_count // 128, 256, 128), F32),
            pltpu.VMEM((lon_count // 128, 256, 128), F32),
            pltpu.VMEM((waves // 128, 256, 128), F32),
            pltpu.VMEM((hidden, w_in.shape[0]), BF16),
            pltpu.VMEM((hidden, hidden), BF16),
            pltpu.VMEM((w_out.shape[1], hidden), BF16),
            per_unit, per_unit,
            pltpu.VMEM((fields, WAVES), F32),
            pltpu.VMEM((fields, WAVES), F32),
            per_unit,
            pltpu.VMEM((hidden, hidden), F32),
            per_unit, per_unit, per_unit,
            pltpu.VMEM((members // 2, hidden // (members // 2), 768), BF16),
            pltpu.VMEM((members // 2, hidden // (members // 2), 768), BF16),
            pltpu.VMEM((levels, 16, 384), BF16),
            pltpu.VMEM((levels, 16, 384), BF16),
            pltpu.VMEM((16, 384), BF16),
            pltpu.VMEM((16, 384), BF16),
            dma((2, blocks)), dma(()), dma((len(given),)),
            dma(()), dma((blocks,)), dma(()), dma((blocks // 2,)), dma(()), dma((blocks,)),
            dma(()), dma(()), dma(()), dma(()), dma(()), dma(()), dma(()), dma(()),
        ],
        compiler_params=pltpu.CompilerParams(
            collective_id=0, has_side_effects=True, vmem_limit_bytes=VMEM_LIMIT
        ),
    )(
        shift, visc, ns,
        *[pltpu.with_memory_space_constraint(x, pltpu.HBM)
          for x in (state.reshape(flat), noise.reshape(flat), cot.reshape(flat), *given)],
    )
    out = pl.pallas_call(
        functools.partial(finish, hidden, levels, members),
        name="finish",
        out_shape=(
            jax.ShapeDtypeStruct(flat, F32),
            jax.ShapeDtypeStruct(flat, F32),
            jax.ShapeDtypeStruct((own, w_in.shape[0]), F32),
            jax.ShapeDtypeStruct((own, hidden), F32),
            jax.ShapeDtypeStruct((own, w_out.shape[1]), F32),
            jax.ShapeDtypeStruct((2, own), F32),
        ),
        in_specs=[vmem, vmem, vmem],
        out_specs=(hbm, hbm, vmem, vmem, vmem, vmem),
        scratch_shapes=[dma((2, fields))],
        compiler_params=pltpu.CompilerParams(vmem_limit_bytes=32 << 20),
    )(state_out, grad_out, sums)
    return (
        out[0].reshape(shape), out[1].reshape(shape), out[2].T, out[3].T, out[4].T, out[5],
    )


def solution(mesh):
    grid = P("member", "level", None, None, None)
    return jax.shard_map(
        functools.partial(per_device, mesh.shape["level"], mesh.shape["member"]),
        mesh=mesh,
        in_specs=(grid, grid, grid, P("level", None), P("level", None), P("level", None))
        + (P(),) * 5,
        out_specs=(grid, grid) + (P(None, ("level", "member")),) * 4,
        check_vma=False,
    )
```

time: 124 us -> 94.6 us (0.76)
  local copies, waits for them, and re-layouts: 14.5 us -> 0 us
  Pallas kernels: 108 us -> 93.9 us
    pallas_call x1, Pallas kernels: 108 us -> 89.8 us  [per_device(): pl.pallas_call(functools.partial(kernel, levels, members, lat_count, lon_...]
    unnamed x10 -> x0, local copies, waits for them, and re-layouts: 12 us -> none
    pallas_call x0 -> x1, Pallas kernels: none -> 4.02 us  [per_device(): pl.pallas_call(functools.partial(finish, hidden, levels, members), name='...]
    reshape x2 -> x0, local copies, waits for them, and re-layouts: 2.49 us -> none  [the longest x1 1.25 us: per_device(): b_in.reshape(1, -1)]
where the time goes in v2:
time: 94.6 us; the launch traced here: 94.5 us
  Pallas kernels  93.9 us (99%)
    pallas_call x1, Pallas kernels, per_device(): pl.pallas_call(functools.partial(kernel, levels, members, lat_count, lon_...  89.8 us
    pallas_call x1, Pallas kernels, per_device(): pl.pallas_call(functools.partial(finish, hidden, levels, members), name='...  4.02 us

profile of v2, /device:TPU:1, one launch (start us, length us, event | category | flops | bytes accessed | tf_op | source)
XLA Modules:
  0.0 94.5 jit_solution(7448520639941715451)
XLA Ops:
  0.6 89.8 %ensemble_step.1 = (f32[8,256,512]{2,1,0:T(8,128)S(1)}, f32[8,256,512]{2,1,0:T(8,128)S(1)}, f32[16,384]{1,0:T(8,128)S(1)}) custom-call(f32[2,4]{1,0:T(2,128)} %shift_ref.1, f32[2,4]{1,0:T(2,128)} %visc_ref.1, f32[2,4]{1,0:T(2,128)} %ns_ref.1, f32[8,256,512]{2,1,0:T(8,128)} %bitcast.8, bf16[8,256,512]{2,1,0:T(8,128)(2,1)} %bitcast.9, ...), custom_call_target="tpu_custom_call" | custom-call | tf_op jit(solution)/shard_map/ensemble_step/pallas_call | solution.py:485
  90.5 4.0 %finish.1 = (f32[8,256,512]{2,1,0:T(8,128)}, f32[8,256,512]{2,1,0:T(8,128)}, f32[3,128]{1,0:T(4,128)}, f32[3,384]{1,0:T(4,128)}, f32[3,128]{1,0:T(4,128)}, /*index=5*/f32[2,3]{1,0:T(2,128)}) custom-call(f32[8,256,512]{2,1,0:T(8,128)S(1)} %get-tuple-element.15.next_in, f32[8,256,512]{2,1,0:T(8,128)S(1)} %get-tuple-element.16.grad_in, ...), custom_call_target="tpu_custom_call" | custom-call | tf_op jit(solution)/shard_map/finish/pallas_call | solution.py:534

commit v3 on v2

--- a/solution.py
+++ b/solution.py
@@ -15,7 +15,8 @@
 F32 = jnp.float32
 BF16 = jnp.bfloat16
 MESH = pl.DeviceIdType.MESH
-EARLY = 3
+EARLY = 2
+STRIDE = 7
 VMEM_LIMIT = 46 << 20
 
 
@@ -104,7 +105,27 @@
             pltpu.make_async_copy(cot_hbm.at[:, rows], cot_v.at[:, rows], in_sem.at[1, a]),
         )
 
-    for a in range(blocks):
+    for copy in load_block(0):
+        copy.start()
+
+    barrier = pltpu.get_barrier_semaphore()
+
+    def greet_level(d, _):
+        pl.semaphore_signal(
+            barrier, inc=1, device_id={"level": lax.rem(me + d, levels)}, device_id_type=MESH
+        )
+        return 0
+
+    columns_x = members // 2
+    my_y, my_x = mem // columns_x, lax.rem(mem, columns_x)
+    beside = [my_y * columns_x + lax.rem(my_x + d, columns_x) for d in range(1, columns_x)]
+    across = (1 - my_y) * columns_x + my_x
+
+    lax.fori_loop(1, levels, greet_level, 0)
+    for to in (*beside, across):
+        pl.semaphore_signal(barrier, inc=1, device_id={"member": to}, device_id_type=MESH)
+
+    for a in range(1, blocks):
         for copy in load_block(a):
             copy.start()
     load_state = pltpu.make_async_copy(state_hbm, state_v, state_sem)
@@ -123,27 +144,9 @@
     for copy in given:
         copy.start()
 
-    barrier = pltpu.get_barrier_semaphore()
-
-    def greet_level(d, _):
-        pl.semaphore_signal(
-            barrier, inc=1, device_id={"level": lax.rem(me + d, levels)}, device_id_type=MESH
-        )
-        return 0
-
-    columns_x = members // 2
-    my_y, my_x = mem // columns_x, lax.rem(mem, columns_x)
-    beside = [my_y * columns_x + lax.rem(my_x + d, columns_x) for d in range(1, columns_x)]
-    across = (1 - my_y) * columns_x + my_x
-
-    lax.fori_loop(1, levels, greet_level, 0)
-    for to in (*beside, across):
-        pl.semaphore_signal(barrier, inc=1, device_id={"member": to}, device_id_type=MESH)
-    pl.semaphore_wait(barrier, levels - 1 + columns_x)
-
     def send_level(src, dst, send, recv):
         def one(d, _):
-            to = lax.rem(me + d, levels)
+            to = lax.rem(me + STRIDE * d, levels)
             pltpu.make_async_remote_copy(
                 src(to), dst, send, recv, device_id={"level": to}, device_id_type=MESH
             ).start()
@@ -164,11 +167,22 @@
             factor = 1.0 + noise_scale(f) * noise_v[f, rows, :].astype(F32)
             put_rows(st_v, pl.ds(f, 32, stride=fields), cot_v[f, rows, :].astype(F32) * factor)
         g16[a] = get_rows(st_v, slice(None), 0, lon_tiles).astype(BF16).reshape(levels, 16, lon_count)
+        return 0
+
+    def send_grad(a, _):
         send_level(lambda to: g16.at[a, pl.ds(to, 1)], rg.at[a, mine], g_send, g_recv.at[a])
         rg[a, mine] = g16[a, mine]
         return 0
 
-    lax.fori_loop(0, blocks, make_grad, 0)
+    def deal_grad(a, _):
+        make_grad(a, 0)
+        return send_grad(a, 0)
+
+    half = blocks // 2
+    make_grad(0, 0)
+    pl.semaphore_wait(barrier, levels - 1 + columns_x)
+    send_grad(0, 0)
+    lax.fori_loop(1, half, deal_grad, 0)
 
     field_row = lax.broadcasted_iota(jnp.int32, (fields, WAVES), 0)
     wave = lax.broadcasted_iota(jnp.int32, (fields, WAVES), 1).astype(F32)
@@ -221,7 +235,14 @@
         rh[two, mine] = h16[two, mine]
         return 0
 
-    lax.fori_loop(0, blocks // 2, pack_rows, 0)
+    lax.fori_loop(0, half // 2, pack_rows, 0)
+
+    def later(b, _):
+        deal_grad(2 * b, 0)
+        deal_grad(2 * b + 1, 0)
+        return pack_rows(b, 0)
+
+    lax.fori_loop(half // 2, half, later, 0)
 
     for copy in given[6:]:
         copy.wait()
@@ -255,8 +276,6 @@
         cot = cot_v[f]
         z_v[f] = dot(cot, lfh_ref[...]) + dot(cot, lfl_ref[...])
         return 0
-
-    lax.fori_loop(0, fields, local, 0)
 
     others = pl.ds(0, levels - 1)
 
@@ -337,6 +356,7 @@
         return 0
 
     lax.fori_loop(0, blocks, columns, 0)
+    lax.fori_loop(EARLY, EARLY + 2, send_tend, 0)
 
     lane = lax.broadcasted_iota(jnp.int32, (hidden, 128), 1)
     bias = jnp.where(lane == 0, jnp.sum(s1_a[...], axis=1, keepdims=True), 0.0)
@@ -350,35 +370,8 @@
             device_id={"member": to}, device_id_type=MESH,
         ).start()
     gx[my_x] = gs[my_x]
-    lax.fori_loop(EARLY, EARLY + 2, send_tend, 0)
-
-    wait_for(bbr.at[:, others], b_recv)
-
-    def gather(a, _):
-        put_rows(b_v, slice(None), bbr[a].astype(F32).reshape(256, waves))
-        rows = pl.ds(pl.multiple_of(a * 32, 32), 32)
-        for f in range(fields):
-            z_v[f, rows, :] += get_rows(b_v, pl.ds(f, 32, stride=fields), 0, wave_tiles)
-        return 0
-
-    lax.fori_loop(0, blocks, gather, 0)
-
-    def backward(f, _):
-        spectrum = dot3(both(at), halves(z_v[f]))
-        cosine, sine = rotation(f)
-        a, b = spectrum[:, :WAVES], spectrum[:, WAVES:]
-        turned = jnp.concatenate([a * cosine + b * sine, b * cosine - a * sine], axis=1)
-        rows = halves(dot3(both(la), halves(turned)))
-        grad_v[f] = dot3(rows, both(lt))
-        late = EARLY + 2 + f // 2
-
-        @pl.when((lax.rem(f, 2) == 0) & (late < blocks))
-        def _():
-            send_tend(late, 0)
-
-        return 0
-
-    lax.fori_loop(0, fields, backward, 0)
+    lax.fori_loop(EARLY + 2, EARLY + 4, send_tend, 0)
+    lax.fori_loop(0, fields, local, 0)
 
     wait_for(gx.at[pl.ds(0, columns_x - 1)], x_recv)
     total = gx[0].astype(F32)
@@ -394,6 +387,36 @@
     gl[...] = jnp.concatenate(pair, axis=1).astype(BF16)
     send_level(lambda to: gl.at[pl.ds(to, 1)], gr.at[mine], s_send, s_recv)
     gr[mine] = gl[mine]
+
+    lax.fori_loop(EARLY + 4, EARLY + 5, send_tend, 0)
+
+    wait_for(bbr.at[:, others], b_recv)
+
+    def gather(a, _):
+        put_rows(b_v, slice(None), bbr[a].astype(F32).reshape(256, waves))
+        rows = pl.ds(pl.multiple_of(a * 32, 32), 32)
+        for f in range(fields):
+            z_v[f, rows, :] += get_rows(b_v, pl.ds(f, 32, stride=fields), 0, wave_tiles)
+        return 0
+
+    lax.fori_loop(0, blocks, gather, 0)
+
+    def backward(f, _):
+        spectrum = dot3(both(at), halves(z_v[f]))
+        cosine, sine = rotation(f)
+        a, b = spectrum[:, :WAVES], spectrum[:, WAVES:]
+        turned = jnp.concatenate([a * cosine + b * sine, b * cosine - a * sine], axis=1)
+        rows = halves(dot3(both(la), halves(turned)))
+        grad_v[f] = dot3(rows, both(lt))
+        late = EARLY + 5 + f // 2
+
+        @pl.when((lax.rem(f, 2) == 0) & (late < blocks))
+        def _():
+            send_tend(late, 0)
+
+        return 0
+
+    lax.fori_loop(0, fields, backward, 0)
 
     def arrive(a, _):
         wait_for(tbr.at[a, others], t_recv.at[a])

time: 94.6 us -> 85.5 us (0.904)
  Pallas kernels: 93.9 us -> 84.7 us
    pallas_call x1, Pallas kernels: 89.8 us -> 80.7 us  [per_device(): pl.pallas_call(functools.partial(kernel, levels, members, lat_count, lon_...]
where the time goes in v3:
time: 85.5 us; the launch traced here: 85.4 us
  Pallas kernels  84.7 us (99%)
    pallas_call x1, Pallas kernels, per_device(): pl.pallas_call(functools.partial(kernel, levels, members, lat_count, lon_...  80.7 us
    pallas_call x1, Pallas kernels, per_device(): pl.pallas_call(functools.partial(finish, hidden, levels, members), name='...  4.02 us

profile of v3, /device:TPU:1, one launch (start us, length us, event | category | flops | bytes accessed | tf_op | source)
XLA Modules:
  0.0 85.4 jit_solution(1566188476234972504)
XLA Ops:
  0.6 80.7 %ensemble_step.1 = (f32[8,256,512]{2,1,0:T(8,128)S(1)}, f32[8,256,512]{2,1,0:T(8,128)S(1)}, f32[16,384]{1,0:T(8,128)S(1)}) custom-call(f32[2,4]{1,0:T(2,128)} %shift_ref.1, f32[2,4]{1,0:T(2,128)} %visc_ref.1, f32[2,4]{1,0:T(2,128)} %ns_ref.1, f32[8,256,512]{2,1,0:T(8,128)} %bitcast.8, bf16[8,256,512]{2,1,0:T(8,128)(2,1)} %bitcast.9, ...), custom_call_target="tpu_custom_call" | custom-call | tf_op jit(solution)/shard_map/ensemble_step/pallas_call | solution.py:508
  81.4 4.0 %finish.1 = (f32[8,256,512]{2,1,0:T(8,128)}, f32[8,256,512]{2,1,0:T(8,128)}, f32[3,128]{1,0:T(4,128)}, f32[3,384]{1,0:T(4,128)}, f32[3,128]{1,0:T(4,128)}, /*index=5*/f32[2,3]{1,0:T(2,128)}) custom-call(f32[8,256,512]{2,1,0:T(8,128)S(1)} %get-tuple-element.15.next_in, f32[8,256,512]{2,1,0:T(8,128)S(1)} %get-tuple-element.16.grad_in, ...), custom_call_target="tpu_custom_call" | custom-call | tf_op jit(solution)/shard_map/finish/pallas_call | solution.py:557

commit v4 on v3

--- a/solution.py
+++ b/solution.py
@@ -121,9 +121,9 @@
     beside = [my_y * columns_x + lax.rem(my_x + d, columns_x) for d in range(1, columns_x)]
     across = (1 - my_y) * columns_x + my_x
 
-    lax.fori_loop(1, levels, greet_level, 0)
     for to in (*beside, across):
         pl.semaphore_signal(barrier, inc=1, device_id={"member": to}, device_id_type=MESH)
+    lax.fori_loop(1, levels, greet_level, 0)
 
     for a in range(1, blocks):
         for copy in load_block(a):
@@ -229,10 +229,9 @@
         for r in range(2):
             rows = pl.ds(pl.multiple_of(b * 512, 512) + 256 * r, 256)
             packed = get_rows(h32, rows, 0, wave_tiles).astype(BF16)
-            h16[2 * b + r] = packed.reshape(levels, 16, waves)
-        two = pl.ds(2 * b, 2)
-        send_level(lambda to: h16.at[two, pl.ds(to, 1)], rh.at[two, mine], h_send, h_recv.at[b])
-        rh[two, mine] = h16[two, mine]
+            h16[b, :, pl.ds(16 * r, 16), :] = packed.reshape(levels, 16, waves)
+        send_level(lambda to: h16.at[b, pl.ds(to, 1)], rh.at[b, mine], h_send, h_recv.at[b])
+        rh[b, mine] = h16[b, mine]
         return 0
 
     lax.fori_loop(0, half // 2, pack_rows, 0)
@@ -306,9 +305,10 @@
 
         @pl.when(lax.rem(a, 2) == 0)
         def _():
-            wait_for(rh.at[pl.ds(a, 2), others], h_recv.at[a // 2])
-
-        spec = rh[a].reshape(levels * 16, waves)
+            wait_for(rh.at[a // 2, others], h_recv.at[a // 2])
+
+        in_pair = pl.ds(pl.multiple_of(16 * lax.rem(a, 2), 16), 16)
+        spec = rh[a // 2, :, in_pair, :].reshape(levels * 16, waves)
         inp = lanes(dot(spec, lth_ref[...]) + dot(spec, ltl_ref[...]))
         gt = lanes(rg[a].reshape(levels * 16, lon_count).astype(F32))
         pre = dot(win_t[...], inp) + jnp.tile(bb1[...], (1, cols // 128))
@@ -336,13 +336,13 @@
         back = jnp.concatenate([back[:, :lon_count], back[:, lon_count:]], axis=0)
         back = dot(back, lfh_ref[...]) + dot(back, lfl_ref[...])
         half = levels * 8
-        bb[a] = rows_of(back[:half], back[half:], waves)
+        bb[a // 2, :, in_pair, :] = rows_of(back[:half], back[half:], waves)
 
         @pl.when(lax.rem(a, 2) == 1)
         def _():
-            two = pl.ds(a - 1, 2)
-            send_level(lambda to: bb.at[two, pl.ds(to, 1)], bbr.at[two, mine], b_send, b_recv)
-            bbr[two, mine] = bb[two, mine]
+            b = a // 2
+            send_level(lambda to: bb.at[b, pl.ds(to, 1)], bbr.at[b, mine], b_send, b_recv)
+            bbr[b, mine] = bb[b, mine]
 
         @pl.when(a < EARLY)
         def _():
@@ -370,7 +370,6 @@
             device_id={"member": to}, device_id_type=MESH,
         ).start()
     gx[my_x] = gs[my_x]
-    lax.fori_loop(EARLY + 2, EARLY + 4, send_tend, 0)
     lax.fori_loop(0, fields, local, 0)
 
     wait_for(gx.at[pl.ds(0, columns_x - 1)], x_recv)
@@ -388,12 +387,13 @@
     send_level(lambda to: gl.at[pl.ds(to, 1)], gr.at[mine], s_send, s_recv)
     gr[mine] = gl[mine]
 
-    lax.fori_loop(EARLY + 4, EARLY + 5, send_tend, 0)
+    lax.fori_loop(EARLY + 2, blocks - 1, send_tend, 0)
 
     wait_for(bbr.at[:, others], b_recv)
 
     def gather(a, _):
-        put_rows(b_v, slice(None), bbr[a].astype(F32).reshape(256, waves))
+        in_pair = pl.ds(pl.multiple_of(16 * lax.rem(a, 2), 16), 16)
+        put_rows(b_v, slice(None), bbr[a // 2, :, in_pair, :].astype(F32).reshape(256, waves))
         rows = pl.ds(pl.multiple_of(a * 32, 32), 32)
         for f in range(fields):
             z_v[f, rows, :] += get_rows(b_v, pl.ds(f, 32, stride=fields), 0, wave_tiles)
@@ -408,12 +408,6 @@
         turned = jnp.concatenate([a * cosine + b * sine, b * cosine - a * sine], axis=1)
         rows = halves(dot3(both(la), halves(turned)))
         grad_v[f] = dot3(rows, both(lt))
-        late = EARLY + 5 + f // 2
-
-        @pl.when((lax.rem(f, 2) == 0) & (late < blocks))
-        def _():
-            send_tend(late, 0)
-
         return 0
 
     lax.fori_loop(0, fields, backward, 0)
@@ -427,7 +421,7 @@
             next_v[f, rows, :] += get_rows(t_v, pl.ds(f, 32, stride=fields), 0, lon_tiles) * factor
         return 0
 
-    lax.fori_loop(0, blocks - 3, arrive, 0)
+    lax.fori_loop(0, half, arrive, 0)
 
     wait_for(gr.at[others], s_recv)
     total = gr[0].astype(F32)
@@ -439,7 +433,8 @@
     )
     swap.start()
 
-    lax.fori_loop(blocks - 3, blocks, arrive, 0)
+    send_tend(blocks - 1, 0)
+    lax.fori_loop(half, blocks, arrive, 0)
 
     swap.wait()
     norm = 1.0 / math.sqrt(members * lat_count * lon_count)
@@ -503,7 +498,7 @@
     given = [w_in, w_mid, w_out, *[jnp.asarray(t) for t in tables(lat_count, lon_count)]]
     given += [jnp.asarray(unit_order(hidden, levels, members)), b_in, b_mid]
     grid_rows = pltpu.VMEM((blocks, levels, 16, lon_count), BF16)
-    wave_rows = pltpu.VMEM((blocks, levels, 16, waves), BF16)
+    wave_rows = pltpu.VMEM((blocks // 2, levels, 32, waves), BF16)
     per_unit = pltpu.VMEM((hidden, 128), F32)
     state_out, grad_out, sums = pl.pallas_call(
         functools.partial(kernel, levels, members, lat_count, lon_count, hidden),

time: 85.5 us -> 85.3 us (level)
  no operation moved by 1% of the time
where the time goes in v4:
time: 85.3 us; the launch traced here: 85.1 us
  Pallas kernels  84.5 us (99%)
    pallas_call x1, Pallas kernels, per_device(): pl.pallas_call(functools.partial(kernel, levels, members, lat_count, lon_...  80.5 us
    pallas_call x1, Pallas kernels, per_device(): pl.pallas_call(functools.partial(finish, hidden, levels, members), name='...  4.02 us

profile of v4, /device:TPU:1, one launch (start us, length us, event | category | flops | bytes accessed | tf_op | source)
XLA Modules:
  0.0 85.1 jit_solution(1694155815496253262)
XLA Ops:
  0.6 80.5 %ensemble_step.1 = (f32[8,256,512]{2,1,0:T(8,128)S(1)}, f32[8,256,512]{2,1,0:T(8,128)S(1)}, f32[16,384]{1,0:T(8,128)S(1)}) custom-call(f32[2,4]{1,0:T(2,128)} %shift_ref.1, f32[2,4]{1,0:T(2,128)} %visc_ref.1, f32[2,4]{1,0:T(2,128)} %ns_ref.1, f32[8,256,512]{2,1,0:T(8,128)} %bitcast.8, bf16[8,256,512]{2,1,0:T(8,128)(2,1)} %bitcast.9, ...), custom_call_target="tpu_custom_call" | custom-call | tf_op jit(solution)/shard_map/ensemble_step/pallas_call | solution.py:503
  81.1 4.0 %finish.1 = (f32[8,256,512]{2,1,0:T(8,128)}, f32[8,256,512]{2,1,0:T(8,128)}, f32[3,128]{1,0:T(4,128)}, f32[3,384]{1,0:T(4,128)}, f32[3,128]{1,0:T(4,128)}, /*index=5*/f32[2,3]{1,0:T(2,128)}) custom-call(f32[8,256,512]{2,1,0:T(8,128)S(1)} %get-tuple-element.15.next_in, f32[8,256,512]{2,1,0:T(8,128)S(1)} %get-tuple-element.16.grad_in, ...), custom_call_target="tpu_custom_call" | custom-call | tf_op jit(solution)/shard_map/finish/pallas_call | solution.py:552

commit v5 on v4

--- a/solution.py
+++ b/solution.py
@@ -15,7 +15,7 @@
 F32 = jnp.float32
 BF16 = jnp.bfloat16
 MESH = pl.DeviceIdType.MESH
-EARLY = 2
+EARLY = 1
 STRIDE = 7
 VMEM_LIMIT = 46 << 20
 

time: 85.3 us -> 87 us (1.020)
  Pallas kernels: 84.5 us -> 86.2 us
    pallas_call x1, Pallas kernels: 80.5 us -> 82.2 us  [per_device(): pl.pallas_call(functools.partial(kernel, levels, members, lat_count, lon_...]
where the time goes in v5:
time: 87 us; the launch traced here: 86.9 us
  Pallas kernels  86.2 us (99%)
    pallas_call x1, Pallas kernels, per_device(): pl.pallas_call(functools.partial(kernel, levels, members, lat_count, lon_...  82.2 us
    pallas_call x1, Pallas kernels, per_device(): pl.pallas_call(functools.partial(finish, hidden, levels, members), name='...  4.02 us

profile of v5, /device:TPU:1, one launch (start us, length us, event | category | flops | bytes accessed | tf_op | source)
XLA Modules:
  0.0 86.9 jit_solution(12295501122491779560)
XLA Ops:
  0.6 82.2 %ensemble_step.1 = (f32[8,256,512]{2,1,0:T(8,128)S(1)}, f32[8,256,512]{2,1,0:T(8,128)S(1)}, f32[16,384]{1,0:T(8,128)S(1)}) custom-call(f32[2,4]{1,0:T(2,128)} %shift_ref.1, f32[2,4]{1,0:T(2,128)} %visc_ref.1, f32[2,4]{1,0:T(2,128)} %ns_ref.1, f32[8,256,512]{2,1,0:T(8,128)} %bitcast.8, bf16[8,256,512]{2,1,0:T(8,128)(2,1)} %bitcast.9, ...), custom_call_target="tpu_custom_call" | custom-call | tf_op jit(solution)/shard_map/ensemble_step/pallas_call | solution.py:503
  82.9 4.0 %finish.1 = (f32[8,256,512]{2,1,0:T(8,128)}, f32[8,256,512]{2,1,0:T(8,128)}, f32[3,128]{1,0:T(4,128)}, f32[3,384]{1,0:T(4,128)}, f32[3,128]{1,0:T(4,128)}, /*index=5*/f32[2,3]{1,0:T(2,128)}) custom-call(f32[8,256,512]{2,1,0:T(8,128)S(1)} %get-tuple-element.15.next_in, f32[8,256,512]{2,1,0:T(8,128)S(1)} %get-tuple-element.16.grad_in, ...), custom_call_target="tpu_custom_call" | custom-call | tf_op jit(solution)/shard_map/finish/pallas_call | solution.py:552
